TPU v7x, 256 devices: a whole 4x4x8 slice. The times are simulated.
256 devices in a mesh: lon: 64 (over x_hi, z, y), lat: 4 (over x_lo, core).
Axes of the slice: x: 4 (x_hi: 2, x_lo: 2; x = x_hi * 2 + x_lo), y: 4, z: 8, core: 2. Of those that a mesh axis runs over, the one named last changes fastest.
Arguments:
- height: float32 [256, 16000], P('lat', 'lon'), may hold values from -6 to 6
- divergence: float32 [256, 16000], P('lat', 'lon'), may hold values from -6 to 6
- depth: float32 [256, 16000], P('lat', 'lon'), may hold values from 0.25 to 4
- tide: float32 [256, 16000], P('lat', 'lon'), may hold values from -6 to 6
- gauss_weight: float32 [128], P('lat'), may hold values from 0.5 to 1.5
- legendre: bfloat16 [1792, 128, 3585], P('lon', 'lat'), may hold values from -4 to 4
Outputs:
- height_new: float32 [256, 16000], P('lat', 'lon')
- divergence_new: float32 [256, 16000], P('lat', 'lon')
All inputs are finite; a program needn't handle non-finite values.
Results may differ from a plain program's by a relative error of at most 0.0032.
Values may be sent and summed in bfloat16 or wider, within the bound.
A program may use at most 128 MiB of HBM per device.

v0:
```python
import math

import jax
import jax.numpy as jnp
from jax import lax
from jax.sharding import PartitionSpec as P

time_step = 0.5
drag_step = 0.1
coupling = 2.0
gravity_step = 4.0
section_length = 128
highest = lax.Precision.HIGHEST


def angle_table(first_index, second, period):
    product = first_index[:, None] * second[None, :] % period
    angle_value = product.astype(jnp.float32) * (2.0 * math.pi / period)
    return (jnp.cos(angle_value), jnp.sin(angle_value))


def slot_layout(pair_first, pair_count, wave_count, slot_count):
    pair_index = pair_first + jnp.arange(pair_count, dtype=jnp.int32)
    slot_index = jnp.arange(slot_count, dtype=jnp.int32)[None, :]
    pair_column = pair_index[:, None]
    upper_slot = slot_index >= wave_count - pair_column
    degree = jnp.where(upper_slot, slot_index - 1, pair_column + slot_index)
    parity = jnp.where(upper_slot, (slot_index + pair_column + wave_count) % 2, slot_index % 2)
    eigen_value = (
        degree.astype(jnp.float32)
        * (degree + 1).astype(jnp.float32)
        / float(wave_count * wave_count)
    )
    return (upper_slot, parity, eigen_value)


def helmholtz(height_rhs, div_rhs, eigen_value):
    height_spec = (height_rhs - time_step * div_rhs) / (1.0 + coupling * eigen_value)
    div_spec = div_rhs + gravity_step * eigen_value * height_spec
    return jnp.stack([height_spec, div_spec]).astype(jnp.bfloat16)


def forward_fourier(row_block, wave_count, lon_groups):
    item_count, row_count, lon_total = row_block.shape
    inner_count = lon_total // section_length
    outer_count = -(-wave_count // section_length)
    flat_rows = row_block.reshape(item_count * row_count, section_length, inner_count)
    section_index = jnp.arange(section_length, dtype=jnp.int32)
    inner_index = jnp.arange(inner_count, dtype=jnp.int32)
    outer_index = jnp.arange(outer_count, dtype=jnp.int32)
    first_cos, first_sin = angle_table(section_index, section_index, section_length)
    section_real = jnp.einsum("qab,ak->qkb", flat_rows, first_cos, precision=highest)
    section_imag = -jnp.einsum("qab,ak->qkb", flat_rows, first_sin, precision=highest)
    twist_cos, twist_sin = angle_table(section_index, inner_index, lon_total)
    turned_real = section_real * twist_cos + section_imag * twist_sin
    turned_imag = section_imag * twist_cos - section_real * twist_sin
    second_cos, second_sin = angle_table(inner_index, outer_index, inner_count)
    wave_real = jnp.einsum("qkb,bt->qtk", turned_real, second_cos, precision=highest) + jnp.einsum(
        "qkb,bt->qtk", turned_imag, second_sin, precision=highest
    )
    wave_imag = jnp.einsum("qkb,bt->qtk", turned_imag, second_cos, precision=highest) - jnp.einsum(
        "qkb,bt->qtk", turned_real, second_sin, precision=highest
    )
    lon_scale = 1.0 / lon_total
    wave_real = wave_real.reshape(item_count * row_count, outer_count * section_length) * lon_scale
    wave_imag = wave_imag.reshape(item_count * row_count, outer_count * section_length) * lon_scale
    half_count = wave_count // 2
    pair_count = half_count // lon_groups

    def arrange(values):
        lower_part = values[:, :half_count].reshape(-1, lon_groups, pair_count)
        upper_part = values[:, half_count:][:, ::-1].reshape(-1, lon_groups, pair_count)
        return jnp.stack([lower_part, upper_part], axis=2)

    packed = jnp.stack([arrange(wave_real), arrange(wave_imag)], axis=2)
    return packed.reshape(item_count, row_count, lon_groups * 4 * pair_count)


def inverse_fourier(packed, wave_count, lon_groups, lon_total):
    item_count, row_count, width_count = packed.shape
    half_count = wave_count // 2
    pair_count = half_count // lon_groups
    split_form = packed.reshape(item_count * row_count, lon_groups, 2, 2, pair_count)
    lower_part = jnp.transpose(split_form[:, :, :, 0], (0, 2, 1, 3)).reshape(-1, 2, half_count)
    upper_part = jnp.transpose(split_form[:, :, :, 1], (0, 2, 1, 3)).reshape(-1, 2, half_count)[
        :, :, ::-1
    ]
    ordered = jnp.concatenate([lower_part, upper_part], axis=2)
    wave_index = jnp.arange(wave_count, dtype=jnp.int32)
    factor = jnp.where(wave_index == 0, 1.0, 2.0).astype(jnp.float32)
    inner_count = lon_total // section_length
    outer_count = -(-wave_count // section_length)
    coef_real = (ordered[:, 0] * factor).reshape(-1, outer_count, section_length)
    coef_imag = (ordered[:, 1] * factor).reshape(-1, outer_count, section_length)
    section_index = jnp.arange(section_length, dtype=jnp.int32)
    inner_index = jnp.arange(inner_count, dtype=jnp.int32)
    outer_index = jnp.arange(outer_count, dtype=jnp.int32)
    second_cos, second_sin = angle_table(outer_index, inner_index, inner_count)
    part_real = jnp.einsum("qtk,tb->qkb", coef_real, second_cos, precision=highest) - jnp.einsum(
        "qtk,tb->qkb", coef_imag, second_sin, precision=highest
    )
    part_imag = jnp.einsum("qtk,tb->qkb", coef_real, second_sin, precision=highest) + jnp.einsum(
        "qtk,tb->qkb", coef_imag, second_cos, precision=highest
    )
    twist_cos, twist_sin = angle_table(section_index, inner_index, lon_total)
    turned_real = part_real * twist_cos - part_imag * twist_sin
    turned_imag = part_real * twist_sin + part_imag * twist_cos
    first_cos, first_sin = angle_table(section_index, section_index, section_length)
    grid_rows = jnp.einsum("qkb,ak->qab", turned_real, first_cos, precision=highest) - jnp.einsum(
        "qkb,ak->qab", turned_imag, first_sin, precision=highest
    )
    return grid_rows.reshape(item_count, row_count, lon_total)


def per_device(height, divergence, depth, tide, gauss_weight, legendre):
    lon_groups = lax.axis_size("lon")
    lat_groups = lax.axis_size("lat")
    pair_count, north_count, slot_count = legendre.shape
    wave_count = 2 * pair_count * lon_groups
    lat_count = 2 * north_count * lat_groups
    lon_total = height.shape[1] * lon_groups
    norm_factor = math.sqrt(lon_total / lat_count) / wave_count
    forcing = jnp.stack(
        [
            height - time_step * (depth - 1.0) * divergence,
            divergence * (1.0 - drag_step / depth),
            tide,
        ]
    )
    spread = forward_fourier(
        lax.all_to_all(forcing, "lon", split_axis=1, concat_axis=2, tiled=True),
        wave_count,
        lon_groups,
    )
    band_waves = lax.all_to_all(spread, "lon", split_axis=2, concat_axis=1, tiled=True)
    band_form = band_waves.reshape(3, 2, north_count, 2, 2, pair_count)
    weight = (gauss_weight * norm_factor)[None, :, None, None, None]
    even_part = (band_form[:, 0] + band_form[:, 1]) * weight
    odd_part = (band_form[:, 0] - band_form[:, 1]) * weight
    folded = jnp.stack([even_part, odd_part], axis=1).astype(jnp.bfloat16)
    lat_sums = jnp.einsum(
        "ijk,fqjrai->afqrik", legendre, folded, preferred_element_type=jnp.float32
    )
    upper_slot, parity, eigen_value = slot_layout(
        lax.axis_index("lon") * pair_count, pair_count, wave_count, slot_count
    )
    odd_slot = parity == 1
    lower_slot = jnp.logical_not(upper_slot)
    even_slot = jnp.logical_not(odd_slot)
    select_masks = jnp.stack(
        [
            jnp.stack([lower_slot & even_slot, lower_slot & odd_slot]),
            jnp.stack([upper_slot & even_slot, upper_slot & odd_slot]),
        ]
    ).astype(jnp.float32)
    spectral = jnp.einsum("aqik,afqrik->frik", select_masks, lat_sums, precision=highest)
    summed = lax.psum(spectral, "lat")
    div_rhs = summed[1] - gravity_step * eigen_value * summed[2]
    solved = helmholtz(summed[0], div_rhs, eigen_value)
    member_masks = jnp.stack([lower_slot, upper_slot]).astype(jnp.bfloat16)
    parity_masks = jnp.stack([even_slot, odd_slot]).astype(jnp.bfloat16)
    masked = (
        solved[None, None] * member_masks[:, None, None, None] * parity_masks[None, :, None, None]
    )
    slot_sums = jnp.einsum(
        "ijk,aqfrik->fqjrai", legendre, masked, preferred_element_type=jnp.float32
    )
    north_part = slot_sums[:, 0] + slot_sums[:, 1]
    south_part = slot_sums[:, 0] - slot_sums[:, 1]
    grid_waves = jnp.stack([north_part, south_part], axis=1).reshape(
        2, 2 * north_count, 4 * pair_count
    )
    lon_rows = inverse_fourier(
        lax.all_to_all(grid_waves, "lon", split_axis=1, concat_axis=2, tiled=True),
        wave_count,
        lon_groups,
        lon_total,
    )
    new_fields = lax.all_to_all(lon_rows, "lon", split_axis=2, concat_axis=1, tiled=True)
    return (new_fields[0], new_fields[1])


def solution(mesh):
    in_specs = (
        P("lat", "lon"),
        P("lat", "lon"),
        P("lat", "lon"),
        P("lat", "lon"),
        P("lat"),
        P("lon", "lat", None),
    )
    out_specs = (P("lat", "lon"), P("lat", "lon"))
    return jax.shard_map(
        per_device, mesh=mesh, in_specs=in_specs, out_specs=out_specs, check_vma=False
    )
```

profile of v0, /device:TPU:2, one launch (start us, length us, event | category | flops | bytes accessed | tf_op | source)
XLA Modules:
  0.0 645.6 jit_solution(13168154059006172092)
XLA Ops:
  7.2 0.9 stack.74
  8.1 0.9 multiply_subtract_fusion.1
  9.1 0.9 pad_maximum_fusion.1
  10.0 13.7 %all-to-all-start = ((f32[3,64,250]{2,0,1:T(4,128)}), f32[3,64,250]{2,0,1:T(4,128)S(1)}, u32[]{:S(2)}, u32[]{:S(2)}) async-start(f32[3,64,250]{2,0,1:T(4,128)} %pad_maximum_fusion.1), calls=%async_computation | async-start | bytes 524288 | tf_op jit(solution)/shard_map/all_to_all | solution.py:131
  23.7 2.9 not_and_fusion.1
  26.6 3.0 not_and_fusion.2
  29.6 1.0 add_bitcast_fusion.1
  30.6 1.0 add_bitcast_fusion.2
  31.6 0.9 fusion.5
  32.5 0.9 copy.91
  33.3 0.3 fusion.56
  33.6 4.8 all-to-all-done
  38.6 0.6 convolution_negate_fusion
  39.2 0.6 fusion.47
  39.8 0.4 fusion.24
  40.2 0.4 fusion.28
  40.6 0.4 fusion.15
  41.1 1.2 rev.10
  42.4 0.4 fusion.17
  42.9 1.2 rev.9
  45.5 0.3 copy.64
  45.7 0.6 reshape.830
  46.3 5.7 copy.65
  52.0 0.5 broadcast.873
  52.5 34.1 %reduce.10 = f32[7168,3]{1,0:T(8,128)} reduce(f32[7168,1,3]{2,1,0:T(1,128)} %bitcast.112, f32[]{:T(128)} %broadcast.873), dimensions={1}, to_apply=%bitcast.101.reduce_sub_computation | reduce | bytes 172036
  86.6 4.3 reshape.853
  90.9 8.0 %all-to-all-start.1 = ((f32[64,1,336]{2,1,0:T(1,128)}), f32[64,1,336]{2,1,0:T(1,128)S(1)}, u32[]{:S(2)}, u32[]{:S(2)}) async-start(f32[64,1,336]{2,1,0:T(1,128)} %reshape.853), calls=%async_computation.1 | async-start | bytes 196608 | tf_op jit(solution)/shard_map/all_to_all | solution.py:135
  99.0 12.4 %all-to-all-done.1 = f32[64,1,336]{2,1,0:T(1,128)S(1)} async-done(((f32[64,1,336]{2,1,0:T(1,128)}), f32[64,1,336]{2,1,0:T(1,128)S(1)}, u32[]{:S(2)}, u32[]{:S(2)}) %all-to-all-start.1) | async-done | bytes 86048 | tf_op jit(solution)/shard_map/all_to_all | solution.py:135
  111.4 0.9 reduce.11
  112.3 6.9 %reshape.854 = f32[7168,1,3]{2,1,0:T(1,128)} reshape(f32[64,336]{1,0:T(8,128)S(1)} %reduce.11) | data formatting | bytes 172032
  119.2 7.3 %copy.66 = f32[3,1,7168]{2,0,1:T(4,128)S(1)} copy(f32[3,1,7168]{0,1,2:T(1,128)} %bitcast.111) | data formatting | bytes 172032 | tf_op jit(solution)/shard_map/all_to_all | solution.py:135
  126.5 0.7 reshape.831
  127.8 19.6 %fusion = f32[28,3585,3,2]{1,3,2,0:T(2,128)} fusion(bf16[28,32,3585]{2,1,0:T(8,128)(2,1)} %param.11, f32[28,3585,2,2]{1,2,3,0:T(2,128)S(1)} %copy.91, bf16[3,1,32,2,2,28]{2,4,3,1,0,5:T(2,128)(2,1)S(1)} %get-tuple-element.17, bf16[3,1,32,2,2,28]{2,4,3,1,0,5:T(2,128)(2,1)S(1)} %get-tuple-element.16), kind=kOutput, calls=%fused_computation.1 | convolution fusion | flops 158485664 | bytes 10482528 | tf_op jit(solution)/shard_map/ijk,fqjrai->afqrik/dot_general | solution.py:141
  147.5 2.0 add_convert_fusion.1
  149.6 1.0 add_convert_fusion
  150.5 0.2 fusion.20
  150.8 57.6 %all-reduce.2.cloned.1.call-done = f32[3,2,28,3585]{3,1,0,2:T(2,128)} async-done(((f32[3,2,28,3585]{3,1,0,2:T(2,128)}), f32[3,2,28,3585]{3,1,0,2:T(2,128)}) %all-reduce.2.cloned.1.call-update) | async-done | bytes 2409136 | tf_op jit(solution)/shard_map/psum | solution.py:157
  208.4 2.7 fusion.182
  211.1 0.8 add_convert_fusion.2
  211.9 1.1 pad_maximum_fusion
  213.0 1.8 broadcast_multiply_fusion
  214.8 7.6 %fusion.8 = f32[2,2,32,2,2,28]{2,3,0,1,4,5:T(2,128)S(1)} fusion(bf16[28,32,3585]{2,1,0:T(8,128)(2,1)} %param.11, bf16[2,28,3585]{2,0,1:T(2,128)(2,1)S(1)} %add_convert_fusion.1, bf16[2,2,2,28,3585]{4,2,1,0,3:T(2,128)(2,1)S(1)} %broadcast_multiply_fusion), kind=kOutput, calls=%fused_computation.19 | convolution fusion | flops 109213440 | bytes 8489264 | tf_op jit(solution)/shard_map/ijk,aqfrik->fqjrai/dot_general | solution.py:165
  222.7 0.3 copy.87
  223.0 0.9 reshape.848
  223.9 13.4 %all-to-all-start.2 = ((f32[2,64,112]{2,0,1:T(2,128)}), f32[2,64,112]{2,0,1:T(2,128)S(1)}, u32[]{:S(2)}, u32[]{:S(2)}) async-start(f32[2,64,112]{2,0,1:T(2,128)} %reshape.848), calls=%async_computation.2 | async-start | bytes 131072 | tf_op jit(solution)/shard_map/all_to_all | solution.py:174
  237.3 12.3 %all-to-all-done.2 = f32[2,64,112]{2,0,1:T(2,128)S(1)} async-done(((f32[2,64,112]{2,0,1:T(2,128)}), f32[2,64,112]{2,0,1:T(2,128)S(1)}, u32[]{:S(2)}, u32[]{:S(2)}) %all-to-all-start.2) | async-done | bytes 57376 | tf_op jit(solution)/shard_map/all_to_all | solution.py:174
  250.2 1.3 rev.11
  251.4 0.2 fusion.75
  251.7 0.4 fusion.70
  252.1 0.4 fusion.72
  252.5 0.4 convolution_add_fusion
  252.9 0.4 convolution_subtract_fusion.1
  253.4 0.5 fusion.36
  253.9 0.5 fusion.13
  254.4 0.3 reshape.836
  254.7 11.8 %copy.74 = f32[2,1,16000]{0,1,2:T(1,128)} copy(f32[2,1,16000]{2,0,1:T(2,128)S(1)} %reshape.836) | data formatting | bytes 256000 | tf_op jit(solution)/shard_map/reshape | solution.py:112
  266.5 72.8 %reduce.12 = f32[16000,2]{1,0:T(8,128)} reduce(f32[16000,1,2]{2,1,0:T(1,128)} %bitcast.110, f32[]{:T(128)} %broadcast.873), dimensions={1}, to_apply=%bitcast.103.reduce_sub_computation | reduce | bytes 256004
  339.3 6.7 %reshape.855 = f32[64,1,500]{2,1,0:T(1,128)S(1)} reshape(f32[16000,2]{1,0:T(8,128)} %reduce.12) | data formatting | bytes 256000
  346.0 16.6 %all_to_all.16 = f32[64,1,500]{2,1,0:T(1,128)S(1)} all-to-all(f32[64,1,500]{2,1,0:T(1,128)S(1)} %reshape.855), channel_id=1, replica_groups=mesh['lon'=64,'lat'=4] {'lon'}, dimensions={0} | all-to-all | bytes 256000 | tf_op jit(solution)/shard_map/all_to_all | solution.py:179
  362.6 1.0 reduce.13
  363.5 10.4 %reshape.856 = f32[16000,1,2]{2,1,0:T(1,128)} reshape(f32[64,500]{1,0:T(8,128)S(1)} %reduce.13) | data formatting | bytes 256000
  374.0 263.0 %slice_reduce_fusion = (f32[16000]{0:T(1024)S(1)}, f32[16000]{0:T(1024)S(1)}) fusion(f32[2,1,16000]{0,1,2:T(1,128)} %bitcast.109), kind=kLoop, calls=%fused_computation.2 | loop fusion | bytes 256000 | tf_op jit(solution)/shard_map/slice | solution.py:180
  636.9 0.8 squeeze.34
  637.8 0.8 squeeze.16
  (46 shorter events, 3.2 us)
Async XLA Ops:
  10.0 28.4 %all-to-all-start = ((f32[3,64,250]{2,0,1:T(4,128)}), f32[3,64,250]{2,0,1:T(4,128)S(1)}, u32[]{:S(2)}, u32[]{:S(2)}) async-start(f32[3,64,250]{2,0,1:T(4,128)} %pad_maximum_fusion.1), calls=%async_computation | async-start | bytes 524288 | tf_op jit(solution)/shard_map/all_to_all | solution.py:131
  86.6 12.4 %copy-start.2 = (f32[32]{0:T(128)S(1)}, f32[32]{0:T(128)}, u32[]{:S(2)}) copy-start(f32[32]{0:T(128)} %param.10) | copy-start | bytes 388
  90.9 20.5 %all-to-all-start.1 = ((f32[64,1,336]{2,1,0:T(1,128)}), f32[64,1,336]{2,1,0:T(1,128)S(1)}, u32[]{:S(2)}, u32[]{:S(2)}) async-start(f32[64,1,336]{2,1,0:T(1,128)} %reshape.853), calls=%async_computation.1 | async-start | bytes 196608 | tf_op jit(solution)/shard_map/all_to_all | solution.py:135
  98.9 109.5 %all-reduce.2.cloned.1.call-start = ((), (), s32[]{:S(2)}) async-start(), calls=%async_computation.4 | async-start | bytes 4988928 | tf_op jit(solution)/shard_map/psum | solution.py:157
  147.5 2.1 copy-start.1
  208.4 2.7 copy-start
  223.9 25.7 %all-to-all-start.2 = ((f32[2,64,112]{2,0,1:T(2,128)}), f32[2,64,112]{2,0,1:T(2,128)S(1)}, u32[]{:S(2)}, u32[]{:S(2)}) async-start(f32[2,64,112]{2,0,1:T(2,128)} %reshape.848), calls=%async_computation.2 | async-start | bytes 131072 | tf_op jit(solution)/shard_map/all_to_all | solution.py:174
Sparse Core Ops, SparseCore 0:
  147.6 60.7 all-reduce.1
where the time goes:
time: 656 us; the launch traced here: 646 us
  local copies, waits for them, and re-layouts  329 us (50%)
  other arithmetic  130 us (20%)
  waiting for transfers between devices  87.1 us (13%)
  starting transfers between devices  35.1 us (5%)
  matrix products  32.8 us (5%)
  blocking collectives  16.6 us (3%)
  between operations  14.7 us (2%)
    slice x1, local copies, waits for them, and re-layouts, per_device(): return (new_fields[0], new_fields[1])  263 us
    unnamed x3, other arithmetic  108 us
    psum x1, waiting for transfers between devices, per_device(): summed = lax.psum(spectral, 'lat')  57.6 us
    unnamed x16, local copies, waits for them, and re-layouts  30.1 us
    dot_general x1, matrix products, per_device(): jnp.einsum('ijk,fqjrai->afqrik', legendre, folded, preferred_element_type...  19.6 us
    all_to_all x1, blocking collectives, per_device(): lax.all_to_all(lon_rows, 'lon', split_axis=2, concat_axis=1, tiled=True)  16.6 us
    all_to_all x1, starting transfers between devices, per_device(): lax.all_to_all(forcing, 'lon', split_axis=1, concat_axis=2, tiled=True)  13.7 us
    all_to_all x1, starting transfers between devices, per_device(): lax.all_to_all(grid_waves, 'lon', split_axis=1, concat_axis=2, tiled=True)  13.4 us
  transfers between devices with their start and end apart: 4, of which 4 were waited for; matrix products, arithmetic and copies ran while one was open for 2% of the time, Pallas kernels for 0%

commit v1 on v0

v1 whole, which is shorter than its diff:
```python
import math

import jax
import jax.numpy as jnp
import ml_dtypes
import numpy as np
from jax import lax
from jax.experimental import pallas as pl
from jax.experimental.pallas import tpu as pltpu
from jax.sharding import PartitionSpec as P

time_step = 0.5
drag_step = 0.1
coupling = 2.0
gravity_step = 4.0

f32, bf16 = jnp.float32, jnp.bfloat16

LON_DEV = 64
SPAN = 250
NLON = LON_DEV * SPAN
PAIRS = 28
MT = 2 * PAIRS * LON_DEV
SLOTS = MT + 1
HALF = 32
NLAT = 256
GROUP = 4
GROUPS = PAIRS // GROUP
TILE = 512
TILES = (SLOTS - 1) // TILE
WIDE = 3840
PART = WIDE // 2


def two_terms(table):
    high = table.astype(ml_dtypes.bfloat16)
    low = (table - high.astype(np.float64)).astype(ml_dtypes.bfloat16)
    return high, low


def tables():
    v = np.arange(128)
    s = np.arange(LON_DEV)
    j = np.arange(256)
    real = (j < SPAN).astype(np.float64)
    tau = np.arange(16)
    first = np.stack([v, MT - 1 - v])
    turn = np.stack([128 * tau, -128 * tau])
    psi = 2 * np.pi * ((first[:, :, None] * s) % LON_DEV) / LON_DEV
    spread = np.stack([np.cos(psi), -np.sin(psi)], axis=1).reshape(512, LON_DEV)
    theta = 2 * np.pi * ((first[:, :, None] * j) % NLON) / NLON
    twist_cos = (np.cos(theta) * real).reshape(256, 256).astype(np.float32)
    twist_sin = (np.sin(theta) * real).reshape(256, 256).astype(np.float32)
    phi = 2 * np.pi * ((turn[:, :, None] * j) % NLON) / NLON
    keep = real * (tau < 14)[:, None]
    cos, sin = np.cos(phi) * keep, np.sin(phi) * keep
    inner = np.concatenate(
        [np.concatenate([cos, sin], axis=2), np.concatenate([-sin, cos], axis=2)], axis=1
    ).reshape(64, 512)
    row = (PAIRS * s) // 128
    pick = np.concatenate([row[:, None] == tau, row[:, None] + 1 == tau]).astype(np.float64)
    back_row = np.concatenate([row, row + 1])
    back_phi = np.stack([back_row, -back_row])[:, :, None] * 128 * j % NLON * (2 * np.pi / NLON)
    cos, sin = 2 * np.cos(back_phi) * real, 2 * np.sin(back_phi) * real
    back = np.concatenate(
        [np.concatenate([cos, sin], axis=2), np.concatenate([-sin, cos], axis=2)], axis=1
    ).reshape(512, 512)
    return (
        *two_terms(spread),
        *two_terms(np.ascontiguousarray(spread.T)),
        twist_cos,
        twist_sin,
        *two_terms(inner),
        pick.astype(ml_dtypes.bfloat16),
        *two_terms(back),
    )


def iota(shape, dim):
    return lax.broadcasted_iota(jnp.int32, shape, dim)


def dot(a, b):
    return lax.dot_general(a, b, (((1,), (0,)), ((), ())), preferred_element_type=f32)


def dot_nt(a, b):
    return lax.dot_general(a, b, (((1,), (1,)), ((), ())), preferred_element_type=f32)


def split(x):
    high = x.astype(bf16)
    return high, (x - high.astype(f32)).astype(bf16)


def three(product, a, b):
    return product(a[0], b[0]) + (product(a[0], b[1]) + product(a[1], b[0]))


def forcing_fields(height, divergence, depth, tide):
    return (
        height - time_step * (depth - 1.0) * divergence,
        divergence * (1.0 - drag_step / depth),
        tide,
    )


def fold(field, weight):
    north, south = field[:HALF], field[HALF:]
    return (north + south) * weight, (north - south) * weight


def lane_masks():
    lane = iota((LON_DEV, 128), 1)
    offset = (iota((LON_DEV, 128), 0) * PAIRS) & 127
    valid = ((lane - offset) & 127) < PAIRS
    return valid & (lane >= offset), valid & (lane < offset)


def forward_row(x, spread, twist, inner, pick):
    x = split(x)
    waves = []
    for member in range(2):
        rows = slice(256 * member, 256 * (member + 1))
        y = three(dot, (spread[0][rows], spread[1][rows]), x)
        re, im = y[:128], y[128:]
        rows = slice(128 * member, 128 * (member + 1))
        cos, sin = twist[0][rows], twist[1][rows]
        z = split(jnp.concatenate([re * cos + im * sin, im * cos - re * sin], axis=1))
        rows = slice(32 * member, 32 * (member + 1))
        waves.append(three(dot_nt, (inner[0][rows], inner[1][rows]), z).astype(bf16))
    stacked = jnp.concatenate(
        [waves[slot % 2][16 * (slot // 2) : 16 * (slot // 2 + 1)] for slot in range(4)], axis=1
    )
    values = dot(pick, stacked)
    straight, wrapped = lane_masks()
    message = None
    for slot in range(4):
        cols = slice(128 * slot, 128 * (slot + 1))
        own = jnp.where(
            straight, values[:LON_DEV, cols], jnp.where(wrapped, values[LON_DEV:, cols], 0.0)
        )
        own = pltpu.roll(own, 32 * slot, 1) if slot else own
        message = own if message is None else message + own
    return message


def column_products(rows, lon):
    r = iota((16 * GROUPS, 128), 0)
    target = lon * PAIRS + 32 * (((r >> 2) & 1) * 2 + ((r >> 3) & 1)) + 4 * (r >> 4) + (r & 3)
    order = (((iota((16 * GROUPS, 128), 1) - target) & 127) == 0).astype(f32).astype(bf16)
    q = dot_nt(order, rows.astype(bf16)).astype(bf16)
    source, lane = iota((64, 256), 0), iota((64, 256), 1)
    same = ((source >> 5) == (lane >> 7)) & ((source & 31) == (lane & 31))
    wide = dot(q, same.astype(f32).astype(bf16))
    own = ((iota(wide.shape, 1) >> 5) & 3) == (iota(wide.shape, 0) & 3)
    return jnp.where(own, wide, 0.0)


def slot_terms(shape, pair_first, slot_first):
    pair = pair_first + (iota(shape, 0) & 3)
    slot = slot_first + iota(shape, 1)
    upper = slot >= MT - pair
    odd = (jnp.where(upper, slot + pair, slot) & 1) == 1
    return pair, slot, upper, odd


def partial_solve(sums, pair_first, slot_first):
    shape = (8, sums.shape[1])
    pair, slot, upper, odd = slot_terms(shape, pair_first, slot_first)
    degree = jnp.where(upper, slot - 1, pair + slot)
    eigen = degree.astype(f32) * (degree + 1).astype(f32) / float(MT * MT)
    fields = []
    for field in range(3):
        block = [
            [sums[((par * 3 + field) * 2 + mem) * 8 :][:8] for mem in range(2)] for par in range(2)
        ]
        fields.append(
            jnp.where(
                upper,
                jnp.where(odd, block[1][1], block[0][1]),
                jnp.where(odd, block[1][0], block[0][0]),
            )
        )
    div_rhs = fields[1] - gravity_step * eigen * fields[2]
    height_spec = (fields[0] - time_step * div_rhs) / (1.0 + coupling * eigen)
    return height_spec, div_rhs + gravity_step * eigen * height_spec


def inverse_rows(solved, pair_first, slot_first):
    base = solved.astype(f32)
    _, _, upper, odd = slot_terms(base.shape, pair_first, slot_first)
    low, high = jnp.where(upper, 0.0, base), jnp.where(upper, base, 0.0)
    return jnp.concatenate(
        [low, high, jnp.where(odd, -low, low), jnp.where(odd, -high, high)], axis=0
    ).astype(bf16)


def own_pair(products):
    lane = iota((HALF, 64), 1) & 3
    total = None
    for pair in range(GROUP):
        term = jnp.where(lane == pair, products[HALF * pair : HALF * (pair + 1)], 0.0)
        total = term if total is None else total + term
    return total


def lane_order(lon, group):
    r, c = iota((64, 512), 0), iota((64, 512), 1)
    slot = ((r >> 2) & 1) * 2 + ((r >> 4) & 1)
    target = lon * PAIRS + 32 * slot + 4 * group + (r & 3)
    same = ((r >> 5) == (c >> 8)) & (((r >> 3) & 1) == ((c >> 7) & 1))
    return (same & (((c - target) & 127) == 0)).astype(f32).astype(bf16)


def inverse_row(c, spread_t, twist, back):
    straight, wrapped = lane_masks()
    mean = (iota((LON_DEV, 128), 0) == 0) & (iota((LON_DEV, 128), 1) == 0)
    total = None
    for member in range(2):
        stack = []
        for part in range(2):
            slot = part * 2 + member
            x = pltpu.roll(c, 128 - 32 * slot, 1) if slot else c
            if member == 0:
                x = jnp.where(mean, 0.5 * x, x)
            stack += [jnp.where(straight, x, 0.0), jnp.where(wrapped, x, 0.0)]
        x = split(jnp.concatenate(stack, axis=0).T)
        rows = slice(256 * member, 256 * (member + 1))
        b = three(dot, x, (back[0][rows], back[1][rows]))
        re, im = b[:, :256], b[:, 256:]
        rows = slice(128 * member, 128 * (member + 1))
        cos, sin = twist[0][rows], twist[1][rows]
        z = split(jnp.concatenate([re * cos - im * sin, re * sin + im * cos], axis=0))
        cols = slice(256 * member, 256 * (member + 1))
        term = three(dot, (spread_t[0][:, cols], spread_t[1][:, cols]), z)
        total = term if total is None else total + term
    return total


def kernel(
    height, divergence, depth, tide, weight_row,
    spread_h, spread_l, spread_th, spread_tl, twist_c, twist_s, inner_h, inner_l, pick, back_h, back_l,
    legendre,
    out_height, out_divergence,
    table, field_buf, tx1, rx1, tx2, rx2, tx4, rx4, tx5, rx5,
    columns, sums, sibling_sums, chip_tx, chip_rx, solved, message,
    table_sem, send_sem, recv_sem, own_sem, lat_send, lat_recv,
):
    lon, lat = lax.axis_index("lon"), lax.axis_index("lat")
    core = lax.rem(lat, 2)
    sibling = {"lat": lat + 1 - 2 * core}
    across = {"lat": lax.rem(lat + 2, 4)}
    mine = pl.multiple_of(core * PART, 128)
    theirs = pl.multiple_of(PART - core * PART, 128)

    def table_copy(g):
        rows = pl.ds(GROUP * g, GROUP)
        return pltpu.make_async_copy(legendre.at[rows], table.at[rows], table_sem.at[g])

    for g in range(GROUPS):
        table_copy(g).start()

    barrier = pltpu.get_barrier_semaphore()

    def greet(i, _):
        pl.semaphore_signal(barrier, 1, device_id={"lon": (lon + i) & (LON_DEV - 1)})
        return 0

    lax.fori_loop(1, LON_DEV, greet, 0)
    pl.semaphore_signal(barrier, 1, device_id=sibling)
    pl.semaphore_signal(barrier, 1, device_id=across)

    def exchange_start(phase, tx, rx):
        n = tx.shape[0] // LON_DEV
        own = pl.ds(lon * n, n)
        pltpu.make_async_copy(tx.at[own], rx.at[own], own_sem.at[phase]).start()

        def send(i, _):
            peer = (lon + i) & (LON_DEV - 1)
            pltpu.make_async_remote_copy(
                tx.at[pl.ds(peer * n, n)],
                rx.at[own],
                send_sem.at[phase],
                recv_sem.at[phase],
                device_id={"lon": peer},
            ).start()
            return 0

        lax.fori_loop(1, LON_DEV, send, 0)

    def exchange_wait(phase, tx, rx):
        n = tx.shape[0] // LON_DEV
        own = pl.ds(lon * n, n)
        rest = pl.ds(0, (LON_DEV - 1) * n)
        pltpu.make_async_copy(tx.at[own], rx.at[own], own_sem.at[phase]).wait()
        pltpu.make_async_copy(rx.at[rest], rx.at[rest], recv_sem.at[phase]).wait()
        pltpu.make_async_copy(tx.at[rest], tx.at[rest], send_sem.at[phase]).wait()

    weight = jnp.sum(
        jnp.where(
            iota((HALF, HALF), 0) == iota((HALF, HALF), 1),
            jnp.broadcast_to(weight_row[...], (HALF, HALF)),
            0.0,
        ),
        axis=1,
        keepdims=True,
    ) * (math.sqrt(NLON / NLAT) / MT / NLON)
    field_buf[...] = jnp.zeros_like(field_buf)
    fields = forcing_fields(height[...], divergence[...], depth[...], tide[...])
    for f in range(3):
        even, odd = fold(fields[f], weight)
        field_buf[0:HALF, 0:SPAN] = even
        field_buf[HALF:, 0:SPAN] = odd
        for h in range(2):
            tx1[pl.ds(2 * f + h, LON_DEV, stride=6), :] = field_buf[:, 128 * h : 128 * (h + 1)]

    pl.semaphore_wait(barrier, LON_DEV + 1)
    exchange_start(0, tx1, rx1)
    exchange_wait(0, tx1, rx1)

    spread = (spread_h, spread_l)
    twist = (twist_c, twist_s)
    inner = (inner_h, inner_l)
    for f in range(3):
        x = jnp.concatenate([rx1[pl.ds(2 * f + h, LON_DEV, stride=6), :] for h in range(2)], axis=1)
        tx2[pl.ds(f, LON_DEV, stride=3), :] = forward_row(x, spread, twist, inner, pick[...])
    exchange_start(1, tx2, rx2)
    exchange_wait(1, tx2, rx2)

    for f in range(3):
        wide = column_products(rx2[pl.ds(f, LON_DEV, stride=3), :], lon).astype(bf16)
        for g in range(GROUPS):
            for par in range(2):
                columns[g, 16 * (par * 3 + f) : 16 * (par * 3 + f + 1), :] = wide[
                    16 * g : 16 * (g + 1), 128 * par : 128 * (par + 1)
                ]

    def table_tail(g):
        last = table[pl.ds(GROUP * g, GROUP), :, SLOTS - 1 : SLOTS].reshape(128, 1).astype(f32)
        return jnp.where(iota((128, 128), 1) == 0, jnp.broadcast_to(last, (128, 128)), 0.0).astype(
            bf16
        )

    def table_tile(g, t):
        return table[pl.ds(GROUP * g, GROUP), :, TILE * t : TILE * (t + 1)].reshape(128, TILE)

    def tiles(g):
        for t in range(TILES):
            yield TILE * t, TILE, table_tile(g, t)
        yield TILE * TILES, 128, table_tail(g)

    def sibling_copy(g):
        return pltpu.make_async_remote_copy(
            sums.at[g, :, pl.ds(theirs, PART)],
            sibling_sums.at[g],
            lat_send.at[0, g],
            lat_recv.at[0, g],
            device_id=sibling,
        )

    def across_copy(g):
        return pltpu.make_async_remote_copy(
            chip_tx.at[g], chip_rx.at[g], lat_send.at[1, g], lat_recv.at[1, g], device_id=across
        )

    def share_copy(g):
        return pltpu.make_async_remote_copy(
            solved.at[g, :, pl.ds(mine, PART)],
            solved.at[g, :, pl.ds(mine, PART)],
            lat_send.at[2, g],
            lat_recv.at[2, g],
            device_id=sibling,
        )

    def forward_group(g):
        table_copy(g).wait()
        pair_first = lon * PAIRS + GROUP * g
        for first, width, rhs in tiles(g):
            both = partial_solve(dot(columns[g], rhs), pair_first, first)
            sums[g, 0:8, first : first + width] = both[0]
            sums[g, 8:16, first : first + width] = both[1]
        sums[g, :, WIDE - 128 : WIDE] = jnp.zeros((16, 128), f32)
        sibling_copy(g).start()

    def sibling_sum(g):
        sibling_copy(g).wait()
        total = sums[g, :, pl.ds(mine, PART)] + sibling_sums[g]
        sibling_sums[g] = total
        chip_tx[g] = total.astype(bf16)
        across_copy(g).start()

    def across_sum(g):
        across_copy(g).wait()
        total = sibling_sums[g] + chip_rx[g].astype(f32)
        solved[g, :, pl.ds(mine, PART)] = total.astype(bf16)
        share_copy(g).start()

    def inverse_group(g):
        share_copy(g).wait()
        pair_first = lon * PAIRS + GROUP * g
        total = None
        for first, width, rhs in tiles(g):
            rows = inverse_rows(solved[g, :, first : first + width], pair_first, first)
            term = dot_nt(rhs, rows)
            total = term if total is None else total + term
        high, low = split(own_pair(total))
        order = lane_order(lon, g)
        message[...] += dot(high, order) + dot(low, order)

    def forward_step(t, _):
        forward_group(t)

        @pl.when(t > 0)
        def _():
            sibling_sum(t - 1)

        return 0

    lax.fori_loop(0, GROUPS, forward_step, 0)
    sibling_sum(GROUPS - 1)

    message[...] = jnp.zeros_like(message)
    across_sum(0)

    def inverse_step(t, _):
        @pl.when(t + 1 < GROUPS)
        def _():
            across_sum(t + 1)

        inverse_group(t)
        return 0

    lax.fori_loop(0, GROUPS, inverse_step, 0)

    for field in range(2):
        for side in range(2):
            tx4[pl.ds(2 * HALF * side + field, HALF, stride=2), :] = message[
                :, 128 * (2 * side + field) : 128 * (2 * side + field + 1)
            ]
    exchange_start(2, tx4, rx4)
    exchange_wait(2, tx4, rx4)

    spread_t = (spread_th, spread_tl)
    back = (back_h, back_l)
    for field in range(2):
        grid = inverse_row(rx4[pl.ds(field, LON_DEV, stride=2), :], spread_t, twist, back)
        for h in range(2):
            tx5[pl.ds(2 * field + h, LON_DEV, stride=4), :] = grid[:, 128 * h : 128 * (h + 1)]
    exchange_start(3, tx5, rx5)
    exchange_wait(3, tx5, rx5)
    for field, out in enumerate((out_height, out_divergence)):
        out[:, 0:128] = rx5[pl.ds(2 * field, LON_DEV, stride=4), :]
        out[:, 128:SPAN] = rx5[pl.ds(2 * field + 1, LON_DEV, stride=4), :][:, : SPAN - 128]


def per_device(height, divergence, depth, tide, gauss_weight, legendre):
    consts = [jnp.asarray(t) for t in tables()]
    vmem = pl.BlockSpec(memory_space=pltpu.VMEM)
    grid_shape = jax.ShapeDtypeStruct(height.shape, f32)

    def pair(rows, dtype=f32):
        return [pltpu.VMEM((LON_DEV * rows, 128), dtype)] * 2

    return pl.pallas_call(
        kernel,
        out_shape=(grid_shape, grid_shape),
        in_specs=[vmem] * (5 + len(consts)) + [pl.BlockSpec(memory_space=pl.ANY)],
        out_specs=(vmem, vmem),
        scratch_shapes=[
            pltpu.VMEM((PAIRS, HALF, SLOTS), bf16),
            pltpu.VMEM((2 * HALF, 256), f32),
            *pair(6),
            *pair(3),
            *pair(2),
            *pair(4),
            pltpu.VMEM((GROUPS, 96, 128), bf16),
            pltpu.VMEM((GROUPS, 16, WIDE), f32),
            pltpu.VMEM((GROUPS, 16, PART), f32),
            pltpu.VMEM((GROUPS, 16, PART), bf16),
            pltpu.VMEM((GROUPS, 16, PART), bf16),
            pltpu.VMEM((GROUPS, 16, WIDE), bf16),
            pltpu.VMEM((HALF, 512), f32),
            pltpu.SemaphoreType.DMA((GROUPS,)),
            pltpu.SemaphoreType.DMA((4,)),
            pltpu.SemaphoreType.DMA((4,)),
            pltpu.SemaphoreType.DMA((4,)),
            pltpu.SemaphoreType.DMA((3, GROUPS)),
            pltpu.SemaphoreType.DMA((3, GROUPS)),
        ],
        compiler_params=pltpu.CompilerParams(
            collective_id=0, has_side_effects=True, vmem_limit_bytes=48 << 20
        ),
    )(height, divergence, depth, tide, gauss_weight.reshape(1, HALF), *consts, legendre)


def solution(mesh):
    in_specs = (
        P("lat", "lon"),
        P("lat", "lon"),
        P("lat", "lon"),
        P("lat", "lon"),
        P("lat"),
        P("lon", "lat", None),
    )
    out_specs = (P("lat", "lon"), P("lat", "lon"))
    return jax.shard_map(
        per_device, mesh=mesh, in_specs=in_specs, out_specs=out_specs, check_vma=False
    )
```

time: 656 us -> 80.4 us (0.12); the launches traced: 646 us -> 79.7 us
  local copies, waits for them, and re-layouts: 329 us -> 15.2 us
  other arithmetic: 130 us -> 0 us
  waiting for transfers between devices: 87.1 us -> 0 us
  Pallas kernels: 0 us -> 63.8 us
  starting transfers between devices: 35.1 us -> 0 us
  matrix products: 32.8 us -> 0 us
  blocking collectives: 16.6 us -> 0 us
  between operations: 14.7 us -> 0.66 us
    slice x4 -> x0, local copies, waits for them, and re-layouts: 263 us -> none  [the longest x1 263 us: per_device(): return (new_fields[0], new_fields[1])]
    unnamed x3 -> x0, other arithmetic: 108 us -> none
    pallas_call x0 -> x1, Pallas kernels: none -> 63.8 us  [per_device(): pl.pallas_call(kernel, out_shape=(grid_shape, grid_shape), in_specs=[vmem...]
    psum x1 -> x0, waiting for transfers between devices: 57.6 us -> none  [per_device(): summed = lax.psum(spectral, 'lat')]
    all_to_all x3 -> x0, starting transfers between devices: 35.1 us -> none  [the longest x1 13.7 us: per_device(): lax.all_to_all(forcing, 'lon', split_axis=1, concat_axis=2, tiled=True)]
    dot_general x14 -> x0, matrix products: 32.8 us -> none  [the longest x1 19.6 us: per_device(): jnp.einsum('ijk,fqjrai->afqrik', legendre, folded, preferred_element_type...]
    all_to_all x3 -> x0, waiting for transfers between devices: 29.5 us -> none  [the longest x1 12.4 us: per_device(): lax.all_to_all(spread, 'lon', split_axis=2, concat_axis=1, tiled=True)]
    reshape x10 -> x0, local copies, waits for them, and re-layouts: 20.5 us -> none  [the longest x2 12 us: inverse_fourier(): return grid_rows.reshape(item_count, row_count, lon_total)]
  transfers between devices with their start and end apart: 4 -> 0, of which waited for: 4 -> 0; matrix products, arithmetic and copies ran while one was open for 2% -> 0% of each run, Pallas kernels for 0% -> 0%
where the time goes in v1:
time: 80.4 us; the launch traced here: 79.7 us
  Pallas kernels  63.8 us (79%)
  local copies, waits for them, and re-layouts  15.2 us (19%)
    pallas_call x1, Pallas kernels, per_device(): pl.pallas_call(kernel, out_shape=(grid_shape, grid_shape), in_specs=[vmem...  63.8 us
    unnamed x34, local copies, waits for them, and re-layouts  15.2 us

profile of v1, /device:TPU:2, one launch (start us, length us, event | category | flops | bytes accessed | tf_op | source)
XLA Modules:
  0.0 79.7 jit_solution(12828088562387102263)
XLA Ops:
  0.6 0.0 copy-start
  0.6 1.0 %copy-done = bf16[512,512]{1,0:T(8,128)(2,1)S(1)} copy-done((bf16[512,512]{1,0:T(8,128)(2,1)S(1)}, bf16[512,512]{1,0:T(8,128)(2,1)}, u32[]{:S(2)}) %copy-start) | copy-done | bytes 524312
  1.7 0.0 copy-start.1
  1.7 1.0 %copy-done.1 = bf16[512,512]{1,0:T(8,128)(2,1)S(1)} copy-done((bf16[512,512]{1,0:T(8,128)(2,1)S(1)}, bf16[512,512]{1,0:T(8,128)(2,1)}, u32[]{:S(2)}) %copy-start.1) | copy-done | bytes 524312
  2.7 0.0 copy-start.2
  2.7 0.9 %copy-done.2 = f32[256,256]{1,0:T(8,128)S(1)} copy-done((f32[256,256]{1,0:T(8,128)S(1)}, f32[256,256]{1,0:T(8,128)}, u32[]{:S(2)}) %copy-start.2) | copy-done | bytes 262168
  3.7 0.0 copy-start.3
  3.7 0.9 %copy-done.3 = f32[256,256]{1,0:T(8,128)S(1)} copy-done((f32[256,256]{1,0:T(8,128)S(1)}, f32[256,256]{1,0:T(8,128)}, u32[]{:S(2)}) %copy-start.3) | copy-done | bytes 262168
  4.6 0.0 copy-start.4
  4.6 0.9 %copy-done.4 = bf16[512,64]{1,0:T(8,128)(2,1)S(1)} copy-done((bf16[512,64]{1,0:T(8,128)(2,1)S(1)}, bf16[512,64]{1,0:T(8,128)(2,1)}, u32[]{:S(2)}) %copy-start.4) | copy-done | bytes 65560
  5.5 0.0 copy-start.5
  5.5 0.9 %copy-done.5 = bf16[512,64]{1,0:T(8,128)(2,1)S(1)} copy-done((bf16[512,64]{1,0:T(8,128)(2,1)S(1)}, bf16[512,64]{1,0:T(8,128)(2,1)}, u32[]{:S(2)}) %copy-start.5) | copy-done | bytes 65560
  6.4 0.0 copy-start.6
  6.4 0.8 %copy-done.6 = f32[64,250]{1,0:T(8,128)S(1)} copy-done((f32[64,250]{1,0:T(8,128)S(1)}, f32[64,250]{1,0:T(8,128)}, u32[]{:S(2)}) %copy-start.6) | copy-done | bytes 64024
  7.3 0.0 copy-start.7
  7.3 0.8 %copy-done.7 = f32[64,250]{1,0:T(8,128)S(1)} copy-done((f32[64,250]{1,0:T(8,128)S(1)}, f32[64,250]{1,0:T(8,128)}, u32[]{:S(2)}) %copy-start.7) | copy-done | bytes 64024
  8.1 0.0 copy-start.8
  8.1 0.8 %copy-done.8 = f32[64,250]{1,0:T(8,128)S(1)} copy-done((f32[64,250]{1,0:T(8,128)S(1)}, f32[64,250]{1,0:T(8,128)}, u32[]{:S(2)}) %copy-start.8) | copy-done | bytes 64024
  8.9 0.0 copy-start.9
  9.0 0.8 %copy-done.9 = f32[64,250]{1,0:T(8,128)S(1)} copy-done((f32[64,250]{1,0:T(8,128)S(1)}, f32[64,250]{1,0:T(8,128)}, u32[]{:S(2)}) %copy-start.9) | copy-done | bytes 64024
  9.8 0.0 copy-start.10
  9.8 0.8 %copy-done.10 = bf16[64,512]{1,0:T(8,128)(2,1)S(1)} copy-done((bf16[64,512]{1,0:T(8,128)(2,1)S(1)}, bf16[64,512]{1,0:T(8,128)(2,1)}, u32[]{:S(2)}) %copy-start.10) | copy-done | bytes 65560
  10.6 0.0 copy-start.11
  10.6 0.8 %copy-done.11 = bf16[64,512]{1,0:T(8,128)(2,1)S(1)} copy-done((bf16[64,512]{1,0:T(8,128)(2,1)S(1)}, bf16[64,512]{1,0:T(8,128)(2,1)}, u32[]{:S(2)}) %copy-start.11) | copy-done | bytes 65560
  11.5 0.0 copy-start.12
  11.5 0.8 %copy-done.12 = bf16[64,512]{1,0:T(8,128)(2,1)S(1)} copy-done((bf16[64,512]{1,0:T(8,128)(2,1)S(1)}, bf16[64,512]{1,0:T(8,128)(2,1)}, u32[]{:S(2)}) %copy-start.12) | copy-done | bytes 65560
  12.3 0.0 copy-start.13
  12.3 0.8 %copy-done.13 = bf16[64,512]{1,0:T(8,128)(2,1)S(1)} copy-done((bf16[64,512]{1,0:T(8,128)(2,1)S(1)}, bf16[64,512]{1,0:T(8,128)(2,1)}, u32[]{:S(2)}) %copy-start.13) | copy-done | bytes 65560
  13.1 0.0 copy-start.14
  13.2 0.8 copy-done.14
  13.9 0.0 copy-start.15
  13.9 0.7 copy-done.15
  14.6 63.8 %shard_map.176 = (f32[64,250]{1,0:T(8,128)S(1)}, f32[64,250]{1,0:T(8,128)S(1)}) custom-call(f32[64,250]{1,0:T(8,128)S(1)} %copy-done.6, f32[64,250]{1,0:T(8,128)S(1)} %copy-done.7, f32[64,250]{1,0:T(8,128)S(1)} %copy-done.8, f32[64,250]{1,0:T(8,128)S(1)} %copy-done.9, f32[1,32]{1,0:T(1,128)S(1)} %bitcast.1, bf16[512,64]{1,0:T(8,128)(2,1)S(1)} %copy-done.5, ...), custom_call_target="tpu_custom_call" | custom-call | tf_op jit(solution)/shard_map/pallas_call | solution.py:465
  78.4 0.6 copy.21
  79.1 0.6 copy.22
Async XLA Ops:
  0.6 1.0 %copy-start = (bf16[512,512]{1,0:T(8,128)(2,1)S(1)}, bf16[512,512]{1,0:T(8,128)(2,1)}, u32[]{:S(2)}) copy-start(bf16[512,512]{1,0:T(8,128)(2,1)} %constant.32.clone.back_l) | copy-start | bytes 1572868
  1.7 1.0 %copy-start.1 = (bf16[512,512]{1,0:T(8,128)(2,1)S(1)}, bf16[512,512]{1,0:T(8,128)(2,1)}, u32[]{:S(2)}) copy-start(bf16[512,512]{1,0:T(8,128)(2,1)} %constant.31.clone.back_h) | copy-start | bytes 1572868
  2.7 0.9 %copy-start.2 = (f32[256,256]{1,0:T(8,128)S(1)}, f32[256,256]{1,0:T(8,128)}, u32[]{:S(2)}) copy-start(f32[256,256]{1,0:T(8,128)} %constant.27.clone.twist_s) | copy-start | bytes 786436
  3.7 0.9 %copy-start.3 = (f32[256,256]{1,0:T(8,128)S(1)}, f32[256,256]{1,0:T(8,128)}, u32[]{:S(2)}) copy-start(f32[256,256]{1,0:T(8,128)} %constant.26.clone.twist_c) | copy-start | bytes 786436
  4.6 0.9 %copy-start.4 = (bf16[512,64]{1,0:T(8,128)(2,1)S(1)}, bf16[512,64]{1,0:T(8,128)(2,1)}, u32[]{:S(2)}) copy-start(bf16[512,64]{1,0:T(8,128)(2,1)} %constant.23.clone.spread_l) | copy-start | bytes 196612
  5.5 0.9 %copy-start.5 = (bf16[512,64]{1,0:T(8,128)(2,1)S(1)}, bf16[512,64]{1,0:T(8,128)(2,1)}, u32[]{:S(2)}) copy-start(bf16[512,64]{1,0:T(8,128)(2,1)} %constant.22.clone.spread_h) | copy-start | bytes 196612
  6.4 0.8 %copy-start.6 = (f32[64,250]{1,0:T(8,128)S(1)}, f32[64,250]{1,0:T(8,128)}, u32[]{:S(2)}) copy-start(f32[64,250]{1,0:T(8,128)} %height.1) | copy-start | bytes 192004
  7.3 0.8 %copy-start.7 = (f32[64,250]{1,0:T(8,128)S(1)}, f32[64,250]{1,0:T(8,128)}, u32[]{:S(2)}) copy-start(f32[64,250]{1,0:T(8,128)} %divergence.1) | copy-start | bytes 192004
  8.1 0.8 %copy-start.8 = (f32[64,250]{1,0:T(8,128)S(1)}, f32[64,250]{1,0:T(8,128)}, u32[]{:S(2)}) copy-start(f32[64,250]{1,0:T(8,128)} %depth.1) | copy-start | bytes 192004
  8.9 0.8 %copy-start.9 = (f32[64,250]{1,0:T(8,128)S(1)}, f32[64,250]{1,0:T(8,128)}, u32[]{:S(2)}) copy-start(f32[64,250]{1,0:T(8,128)} %tide.1) | copy-start | bytes 192004
  9.8 0.8 %copy-start.10 = (bf16[64,512]{1,0:T(8,128)(2,1)S(1)}, bf16[64,512]{1,0:T(8,128)(2,1)}, u32[]{:S(2)}) copy-start(bf16[64,512]{1,0:T(8,128)(2,1)} %constant.29.clone.inner_l) | copy-start | bytes 196612
  10.6 0.8 %copy-start.11 = (bf16[64,512]{1,0:T(8,128)(2,1)S(1)}, bf16[64,512]{1,0:T(8,128)(2,1)}, u32[]{:S(2)}) copy-start(bf16[64,512]{1,0:T(8,128)(2,1)} %constant.28.clone.inner_h) | copy-start | bytes 196612
  11.5 0.8 %copy-start.12 = (bf16[64,512]{1,0:T(8,128)(2,1)S(1)}, bf16[64,512]{1,0:T(8,128)(2,1)}, u32[]{:S(2)}) copy-start(bf16[64,512]{1,0:T(8,128)(2,1)} %constant.25.clone.spread_tl) | copy-start | bytes 196612
  12.3 0.8 %copy-start.13 = (bf16[64,512]{1,0:T(8,128)(2,1)S(1)}, bf16[64,512]{1,0:T(8,128)(2,1)}, u32[]{:S(2)}) copy-start(bf16[64,512]{1,0:T(8,128)(2,1)} %constant.24.clone.spread_th) | copy-start | bytes 196612
  13.1 0.8 copy-start.14
  13.9 0.7 copy-start.15

commit v2 on v1

--- a/solution.py
+++ b/solution.py
@@ -28,8 +28,6 @@
 GROUPS = PAIRS // GROUP
 TILE = 512
 TILES = (SLOTS - 1) // TILE
-WIDE = 3840
-PART = WIDE // 2
 
 
 def two_terms(table):
@@ -39,29 +37,27 @@
 
 
 def tables():
-    v = np.arange(128)
-    s = np.arange(LON_DEV)
-    j = np.arange(256)
+    v, tau, s, j = np.arange(128), np.arange(16), np.arange(LON_DEV), np.arange(256)
     real = (j < SPAN).astype(np.float64)
-    tau = np.arange(16)
-    first = np.stack([v, MT - 1 - v])
-    turn = np.stack([128 * tau, -128 * tau])
-    psi = 2 * np.pi * ((first[:, :, None] * s) % LON_DEV) / LON_DEV
-    spread = np.stack([np.cos(psi), -np.sin(psi)], axis=1).reshape(512, LON_DEV)
+    psi = 2 * np.pi * (np.outer(s, s) % LON_DEV) / LON_DEV
+    spread = np.concatenate([np.cos(psi), -np.sin(psi)])
+    first = np.stack([v, MT - v])
     theta = 2 * np.pi * ((first[:, :, None] * j) % NLON) / NLON
     twist_cos = (np.cos(theta) * real).reshape(256, 256).astype(np.float32)
     twist_sin = (np.sin(theta) * real).reshape(256, 256).astype(np.float32)
-    phi = 2 * np.pi * ((turn[:, :, None] * j) % NLON) / NLON
-    keep = real * (tau < 14)[:, None]
-    cos, sin = np.cos(phi) * keep, np.sin(phi) * keep
+
+    def over_j(row, scale):
+        phi = 2 * np.pi * ((128 * row[..., None] * j) % NLON) / NLON
+        return scale * np.cos(phi) * real, scale * np.sin(phi) * real
+
+    cos, sin = over_j(np.stack([tau, -tau]), 1)
     inner = np.concatenate(
         [np.concatenate([cos, sin], axis=2), np.concatenate([-sin, cos], axis=2)], axis=1
     ).reshape(64, 512)
-    row = (PAIRS * s) // 128
-    pick = np.concatenate([row[:, None] == tau, row[:, None] + 1 == tau]).astype(np.float64)
-    back_row = np.concatenate([row, row + 1])
-    back_phi = np.stack([back_row, -back_row])[:, :, None] * 128 * j % NLON * (2 * np.pi / NLON)
-    cos, sin = 2 * np.cos(back_phi) * real, 2 * np.sin(back_phi) * real
+    row = np.stack([(PAIRS * s) // 128, (PAIRS * s + 1) // 128])
+    row = np.concatenate([row, row + 1], axis=1)
+    pick = (row[..., None] == tau).reshape(256, 16)
+    cos, sin = over_j(row * np.array([[1], [-1]]), 2)
     back = np.concatenate(
         [np.concatenate([cos, sin], axis=2), np.concatenate([-sin, cos], axis=2)], axis=1
     ).reshape(512, 512)
@@ -110,44 +106,48 @@
     return (north + south) * weight, (north - south) * weight
 
 
-def lane_masks():
+def lane_masks(member):
     lane = iota((LON_DEV, 128), 1)
-    offset = (iota((LON_DEV, 128), 0) * PAIRS) & 127
+    offset = (iota((LON_DEV, 128), 0) * PAIRS + member) & 127
     valid = ((lane - offset) & 127) < PAIRS
     return valid & (lane >= offset), valid & (lane < offset)
 
 
+def twice(x):
+    return jnp.concatenate([x, x], axis=0)
+
+
 def forward_row(x, spread, twist, inner, pick):
-    x = split(x)
-    waves = []
+    y = three(dot, spread, split(x))
+    re, im = twice(y[:LON_DEV]), twice(y[LON_DEV:])
+    message = None
     for member in range(2):
-        rows = slice(256 * member, 256 * (member + 1))
-        y = three(dot, (spread[0][rows], spread[1][rows]), x)
-        re, im = y[:128], y[128:]
         rows = slice(128 * member, 128 * (member + 1))
         cos, sin = twist[0][rows], twist[1][rows]
-        z = split(jnp.concatenate([re * cos + im * sin, im * cos - re * sin], axis=1))
-        rows = slice(32 * member, 32 * (member + 1))
-        waves.append(three(dot_nt, (inner[0][rows], inner[1][rows]), z).astype(bf16))
-    stacked = jnp.concatenate(
-        [waves[slot % 2][16 * (slot // 2) : 16 * (slot // 2 + 1)] for slot in range(4)], axis=1
-    )
-    values = dot(pick, stacked)
-    straight, wrapped = lane_masks()
-    message = None
-    for slot in range(4):
-        cols = slice(128 * slot, 128 * (slot + 1))
-        own = jnp.where(
-            straight, values[:LON_DEV, cols], jnp.where(wrapped, values[LON_DEV:, cols], 0.0)
-        )
-        own = pltpu.roll(own, 32 * slot, 1) if slot else own
-        message = own if message is None else message + own
+        if member == 0:
+            z = [re * cos + im * sin, im * cos - re * sin]
+        else:
+            z = [re * cos - im * sin, -(im * cos + re * sin)]
+        z = split(jnp.concatenate(z, axis=1))
+        cols = slice(32 * member, 32 * (member + 1))
+        waves = three(dot_nt, (inner[0][cols], inner[1][cols]), z).astype(bf16)
+        values = dot(pick[rows], jnp.concatenate([waves[:16], waves[16:]], axis=1))
+        straight, wrapped = lane_masks(member)
+        for part in range(2):
+            slot = part * 2 + member
+            cols = slice(128 * part, 128 * (part + 1))
+            own = jnp.where(
+                straight, values[:LON_DEV, cols], jnp.where(wrapped, values[LON_DEV:, cols], 0.0)
+            )
+            own = pltpu.roll(own, 32 * slot, 1) if slot else own
+            message = own if message is None else message + own
     return message
 
 
 def column_products(rows, lon):
     r = iota((16 * GROUPS, 128), 0)
-    target = lon * PAIRS + 32 * (((r >> 2) & 1) * 2 + ((r >> 3) & 1)) + 4 * (r >> 4) + (r & 3)
+    member, part = (r >> 3) & 1, (r >> 2) & 1
+    target = lon * PAIRS + 64 * part + 33 * member + 4 * (r >> 4) + (r & 3)
     order = (((iota((16 * GROUPS, 128), 1) - target) & 127) == 0).astype(f32).astype(bf16)
     q = dot_nt(order, rows.astype(bf16)).astype(bf16)
     source, lane = iota((64, 256), 0), iota((64, 256), 1)
@@ -188,12 +188,11 @@
 
 
 def inverse_rows(solved, pair_first, slot_first):
-    base = solved.astype(f32)
-    _, _, upper, odd = slot_terms(base.shape, pair_first, slot_first)
-    low, high = jnp.where(upper, 0.0, base), jnp.where(upper, base, 0.0)
-    return jnp.concatenate(
-        [low, high, jnp.where(odd, -low, low), jnp.where(odd, -high, high)], axis=0
-    ).astype(bf16)
+    _, _, upper, odd = slot_terms(solved[0].shape, pair_first, slot_first)
+    base = [x.astype(f32) for x in solved]
+    rows = [jnp.where(upper, 0.0, x) for x in base] + [jnp.where(upper, x, 0.0) for x in base]
+    rows += [jnp.where(odd, -x, x) for x in rows]
+    return jnp.concatenate(rows, axis=0).astype(bf16)
 
 
 def own_pair(products):
@@ -207,17 +206,17 @@
 
 def lane_order(lon, group):
     r, c = iota((64, 512), 0), iota((64, 512), 1)
-    slot = ((r >> 2) & 1) * 2 + ((r >> 4) & 1)
-    target = lon * PAIRS + 32 * slot + 4 * group + (r & 3)
+    member, part = (r >> 4) & 1, (r >> 2) & 1
+    target = lon * PAIRS + 64 * part + 33 * member + 4 * group + (r & 3)
     same = ((r >> 5) == (c >> 8)) & (((r >> 3) & 1) == ((c >> 7) & 1))
     return (same & (((c - target) & 127) == 0)).astype(f32).astype(bf16)
 
 
 def inverse_row(c, spread_t, twist, back):
-    straight, wrapped = lane_masks()
     mean = (iota((LON_DEV, 128), 0) == 0) & (iota((LON_DEV, 128), 1) == 0)
     total = None
     for member in range(2):
+        straight, wrapped = lane_masks(member)
         stack = []
         for part in range(2):
             slot = part * 2 + member
@@ -231,63 +230,77 @@
         re, im = b[:, :256], b[:, 256:]
         rows = slice(128 * member, 128 * (member + 1))
         cos, sin = twist[0][rows], twist[1][rows]
-        z = split(jnp.concatenate([re * cos - im * sin, re * sin + im * cos], axis=0))
-        cols = slice(256 * member, 256 * (member + 1))
-        term = three(dot, (spread_t[0][:, cols], spread_t[1][:, cols]), z)
-        total = term if total is None else total + term
-    return total
-
-
-def kernel(
-    height, divergence, depth, tide, weight_row,
-    spread_h, spread_l, spread_th, spread_tl, twist_c, twist_s, inner_h, inner_l, pick, back_h, back_l,
-    legendre,
-    out_height, out_divergence,
-    table, field_buf, tx1, rx1, tx2, rx2, tx4, rx4, tx5, rx5,
-    columns, sums, sibling_sums, chip_tx, chip_rx, solved, message,
-    table_sem, send_sem, recv_sem, own_sem, lat_send, lat_recv,
-):
+        z = [re * cos - im * sin, re * sin + im * cos]
+        z = [part[:LON_DEV] + part[LON_DEV:] for part in z]
+        total = z if total is None else [total[0] + z[0], total[1] - z[1]]
+    return three(dot, spread_t, split(jnp.concatenate(total, axis=0)))
+
+
+CONSTS = 11
+
+
+def kernel(*refs):
+    grid_in, refs = refs[:5], refs[5:]
+    consts_in, refs = refs[:CONSTS], refs[CONSTS:]
+    legendre, out_height, out_divergence, *refs = refs
+    grid, refs = refs[:5], refs[5:]
+    consts, refs = refs[:CONSTS], refs[CONSTS:]
+    table, field_buf, tx1, rx1, tx2, rx2, tx4, rx4, tx5, rx5, *refs = refs
+    columns, sums, sibling_sums, chip_tx, chip_rx, solved, message, *refs = refs
+    in_sem, table_sem, send_sem, recv_sem, own_sem, lat_send, lat_recv = refs
     lon, lat = lax.axis_index("lon"), lax.axis_index("lat")
     core = lax.rem(lat, 2)
     sibling = {"lat": lat + 1 - 2 * core}
     across = {"lat": lax.rem(lat + 2, 4)}
-    mine = pl.multiple_of(core * PART, 128)
-    theirs = pl.multiple_of(PART - core * PART, 128)
+
+    def peers(visit):
+        x, z, y = lon >> 5, (lon >> 2) & 7, lon & 3
+        for step in (4, 3, 5, 2, 6, 1, 7, 0):
+            far = ((z + step) & 7) << 2
+
+            def one(i, _):
+                order = i >> 1
+                turn = jnp.where(order == 0, 2, jnp.where(order == 1, 1, jnp.where(order == 2, 3, 0)))
+                visit(((x ^ (1 - (i & 1))) << 5) | far | ((y + turn) & 3))
+                return 0
+
+            lax.fori_loop(0, 8 if step else 7, one, 0)
 
     def table_copy(g):
         rows = pl.ds(GROUP * g, GROUP)
         return pltpu.make_async_copy(legendre.at[rows], table.at[rows], table_sem.at[g])
 
+    grid_copies = [
+        pltpu.make_async_copy(a, b, in_sem.at[n]) for n, (a, b) in enumerate(zip(grid_in, grid))
+    ]
+    const_copies = [
+        pltpu.make_async_copy(a, b, in_sem.at[5 + n])
+        for n, (a, b) in enumerate(zip(consts_in, consts))
+    ]
+    for copy in grid_copies:
+        copy.start()
+    barrier = pltpu.get_barrier_semaphore()
+    peers(lambda peer: pl.semaphore_signal(barrier, 1, device_id={"lon": peer}))
+    pl.semaphore_signal(barrier, 1, device_id=sibling)
+    pl.semaphore_signal(barrier, 1, device_id=across)
+    for copy in const_copies:
+        copy.start()
     for g in range(GROUPS):
         table_copy(g).start()
-
-    barrier = pltpu.get_barrier_semaphore()
-
-    def greet(i, _):
-        pl.semaphore_signal(barrier, 1, device_id={"lon": (lon + i) & (LON_DEV - 1)})
-        return 0
-
-    lax.fori_loop(1, LON_DEV, greet, 0)
-    pl.semaphore_signal(barrier, 1, device_id=sibling)
-    pl.semaphore_signal(barrier, 1, device_id=across)
 
     def exchange_start(phase, tx, rx):
         n = tx.shape[0] // LON_DEV
         own = pl.ds(lon * n, n)
-        pltpu.make_async_copy(tx.at[own], rx.at[own], own_sem.at[phase]).start()
-
-        def send(i, _):
-            peer = (lon + i) & (LON_DEV - 1)
-            pltpu.make_async_remote_copy(
+        peers(
+            lambda peer: pltpu.make_async_remote_copy(
                 tx.at[pl.ds(peer * n, n)],
                 rx.at[own],
                 send_sem.at[phase],
                 recv_sem.at[phase],
                 device_id={"lon": peer},
             ).start()
-            return 0
-
-        lax.fori_loop(1, LON_DEV, send, 0)
+        )
+        pltpu.make_async_copy(tx.at[own], rx.at[own], own_sem.at[phase]).start()
 
     def exchange_wait(phase, tx, rx):
         n = tx.shape[0] // LON_DEV
@@ -295,8 +308,14 @@
         rest = pl.ds(0, (LON_DEV - 1) * n)
         pltpu.make_async_copy(tx.at[own], rx.at[own], own_sem.at[phase]).wait()
         pltpu.make_async_copy(rx.at[rest], rx.at[rest], recv_sem.at[phase]).wait()
+
+    def exchange_sent(phase, tx):
+        rest = pl.ds(0, (LON_DEV - 1) * (tx.shape[0] // LON_DEV))
         pltpu.make_async_copy(tx.at[rest], tx.at[rest], send_sem.at[phase]).wait()
 
+    for copy in grid_copies:
+        copy.wait()
+    height, divergence, depth, tide, weight_row = grid
     weight = jnp.sum(
         jnp.where(
             iota((HALF, HALF), 0) == iota((HALF, HALF), 1),
@@ -317,14 +336,16 @@
 
     pl.semaphore_wait(barrier, LON_DEV + 1)
     exchange_start(0, tx1, rx1)
+    for copy in const_copies:
+        copy.wait()
+    spread, spread_t, twist, inner, back = (consts[n : n + 2] for n in (0, 2, 4, 6, 9))
+    spread, spread_t = [r[...] for r in spread], [r[...] for r in spread_t]
+    pick = consts[8]
     exchange_wait(0, tx1, rx1)
 
-    spread = (spread_h, spread_l)
-    twist = (twist_c, twist_s)
-    inner = (inner_h, inner_l)
     for f in range(3):
         x = jnp.concatenate([rx1[pl.ds(2 * f + h, LON_DEV, stride=6), :] for h in range(2)], axis=1)
-        tx2[pl.ds(f, LON_DEV, stride=3), :] = forward_row(x, spread, twist, inner, pick[...])
+        tx2[pl.ds(f, LON_DEV, stride=3), :] = forward_row(x, spread, twist, inner, pick)
     exchange_start(1, tx2, rx2)
     exchange_wait(1, tx2, rx2)
 
@@ -352,7 +373,7 @@
 
     def sibling_copy(g):
         return pltpu.make_async_remote_copy(
-            sums.at[g, :, pl.ds(theirs, PART)],
+            sums.at[g, 1 - core],
             sibling_sums.at[g],
             lat_send.at[0, g],
             lat_recv.at[0, g],
@@ -366,8 +387,8 @@
 
     def share_copy(g):
         return pltpu.make_async_remote_copy(
-            solved.at[g, :, pl.ds(mine, PART)],
-            solved.at[g, :, pl.ds(mine, PART)],
+            solved.at[g, core],
+            solved.at[g, core],
             lat_send.at[2, g],
             lat_recv.at[2, g],
             device_id=sibling,
@@ -378,31 +399,30 @@
         pair_first = lon * PAIRS + GROUP * g
         for first, width, rhs in tiles(g):
             both = partial_solve(dot(columns[g], rhs), pair_first, first)
-            sums[g, 0:8, first : first + width] = both[0]
-            sums[g, 8:16, first : first + width] = both[1]
-        sums[g, :, WIDE - 128 : WIDE] = jnp.zeros((16, 128), f32)
+            for field in range(2):
+                sums[g, field, :, first : first + width] = both[field]
         sibling_copy(g).start()
 
     def sibling_sum(g):
-        sibling_copy(g).wait()
-        total = sums[g, :, pl.ds(mine, PART)] + sibling_sums[g]
-        sibling_sums[g] = total
+        sibling_copy(g).wait_recv()
+        total = sums[g, core] + sibling_sums[g]
         chip_tx[g] = total.astype(bf16)
         across_copy(g).start()
+        sibling_sums[g] = total
 
     def across_sum(g):
-        across_copy(g).wait()
+        across_copy(g).wait_recv()
         total = sibling_sums[g] + chip_rx[g].astype(f32)
-        solved[g, :, pl.ds(mine, PART)] = total.astype(bf16)
+        solved[g, core] = total.astype(bf16)
         share_copy(g).start()
 
     def inverse_group(g):
-        share_copy(g).wait()
+        share_copy(g).wait_recv()
         pair_first = lon * PAIRS + GROUP * g
         total = None
         for first, width, rhs in tiles(g):
-            rows = inverse_rows(solved[g, :, first : first + width], pair_first, first)
-            term = dot_nt(rhs, rows)
+            both = [solved[g, field, :, first : first + width] for field in range(2)]
+            term = dot_nt(rhs, inverse_rows(both, pair_first, first))
             total = term if total is None else total + term
         high, low = split(own_pair(total))
         order = lane_order(lon, g)
@@ -441,8 +461,6 @@
     exchange_start(2, tx4, rx4)
     exchange_wait(2, tx4, rx4)
 
-    spread_t = (spread_th, spread_tl)
-    back = (back_h, back_l)
     for field in range(2):
         grid = inverse_row(rx4[pl.ds(field, LON_DEV, stride=2), :], spread_t, twist, back)
         for h in range(2):
@@ -453,21 +471,30 @@
         out[:, 0:128] = rx5[pl.ds(2 * field, LON_DEV, stride=4), :]
         out[:, 128:SPAN] = rx5[pl.ds(2 * field + 1, LON_DEV, stride=4), :][:, : SPAN - 128]
 
+    for phase, tx in enumerate((tx1, tx2, tx4, tx5)):
+        exchange_sent(phase, tx)
+    for g in range(GROUPS):
+        for copy in (sibling_copy, across_copy, share_copy):
+            copy(g).wait_send()
+
 
 def per_device(height, divergence, depth, tide, gauss_weight, legendre):
     consts = [jnp.asarray(t) for t in tables()]
-    vmem = pl.BlockSpec(memory_space=pltpu.VMEM)
+    grid = (height, divergence, depth, tide, gauss_weight.reshape(1, HALF))
+    vmem, hbm = pl.BlockSpec(memory_space=pltpu.VMEM), pl.BlockSpec(memory_space=pltpu.HBM)
     grid_shape = jax.ShapeDtypeStruct(height.shape, f32)
 
-    def pair(rows, dtype=f32):
-        return [pltpu.VMEM((LON_DEV * rows, 128), dtype)] * 2
-
+    def pair(rows):
+        return [pltpu.VMEM((LON_DEV * rows, 128), f32)] * 2
+
+    wide = 128 * pl.cdiv(SLOTS, 128)
     return pl.pallas_call(
         kernel,
         out_shape=(grid_shape, grid_shape),
-        in_specs=[vmem] * (5 + len(consts)) + [pl.BlockSpec(memory_space=pl.ANY)],
+        in_specs=[hbm] * (len(grid) + len(consts) + 1),
         out_specs=(vmem, vmem),
         scratch_shapes=[
+            *[pltpu.VMEM(x.shape, x.dtype) for x in (*grid, *consts)],
             pltpu.VMEM((PAIRS, HALF, SLOTS), bf16),
             pltpu.VMEM((2 * HALF, 256), f32),
             *pair(6),
@@ -475,12 +502,13 @@
             *pair(2),
             *pair(4),
             pltpu.VMEM((GROUPS, 96, 128), bf16),
-            pltpu.VMEM((GROUPS, 16, WIDE), f32),
-            pltpu.VMEM((GROUPS, 16, PART), f32),
-            pltpu.VMEM((GROUPS, 16, PART), bf16),
-            pltpu.VMEM((GROUPS, 16, PART), bf16),
-            pltpu.VMEM((GROUPS, 16, WIDE), bf16),
+            pltpu.VMEM((GROUPS, 2, 8, wide), f32),
+            pltpu.VMEM((GROUPS, 8, wide), f32),
+            pltpu.VMEM((GROUPS, 8, wide), bf16),
+            pltpu.VMEM((GROUPS, 8, wide), bf16),
+            pltpu.VMEM((GROUPS, 2, 8, wide), bf16),
             pltpu.VMEM((HALF, 512), f32),
+            pltpu.SemaphoreType.DMA((5 + CONSTS,)),
             pltpu.SemaphoreType.DMA((GROUPS,)),
             pltpu.SemaphoreType.DMA((4,)),
             pltpu.SemaphoreType.DMA((4,)),
@@ -491,7 +519,7 @@
         compiler_params=pltpu.CompilerParams(
             collective_id=0, has_side_effects=True, vmem_limit_bytes=48 << 20
         ),
-    )(height, divergence, depth, tide, gauss_weight.reshape(1, HALF), *consts, legendre)
+    )(*grid, *consts, legendre)
 
 
 def solution(mesh):

time: 80.4 us -> 75.9 us (0.944)
  Pallas kernels: 63.8 us -> 59.7 us
    pallas_call x1, Pallas kernels: 63.8 us -> 59.7 us  [per_device(): pl.pallas_call(kernel, out_shape=(grid_shape, grid_shape), in_specs=[hbm]...]
where the time goes in v2:
time: 75.9 us; the launch traced here: 75.1 us
  Pallas kernels  59.7 us (79%)
  local copies, waits for them, and re-layouts  14.7 us (19%)
    pallas_call x1, Pallas kernels, per_device(): pl.pallas_call(kernel, out_shape=(grid_shape, grid_shape), in_specs=[hbm]...  59.7 us
    unnamed x34, local copies, waits for them, and re-layouts  14.7 us

profile of v2, /device:TPU:2, one launch (start us, length us, event | category | flops | bytes accessed | tf_op | source)
XLA Modules:
  0.0 75.1 jit_solution(17489481193895411010)
XLA Ops:
  0.6 0.0 copy-start
  0.6 1.0 %copy-done = bf16[512,512]{1,0:T(8,128)(2,1)S(1)} copy-done((bf16[512,512]{1,0:T(8,128)(2,1)S(1)}, bf16[512,512]{1,0:T(8,128)(2,1)}, u32[]{:S(2)}) %copy-start) | copy-done | bytes 524312
  1.7 0.0 copy-start.1
  1.7 1.0 %copy-done.1 = bf16[512,512]{1,0:T(8,128)(2,1)S(1)} copy-done((bf16[512,512]{1,0:T(8,128)(2,1)S(1)}, bf16[512,512]{1,0:T(8,128)(2,1)}, u32[]{:S(2)}) %copy-start.1) | copy-done | bytes 524312
  2.7 0.0 copy-start.2
  2.7 0.9 %copy-done.2 = f32[256,256]{1,0:T(8,128)S(1)} copy-done((f32[256,256]{1,0:T(8,128)S(1)}, f32[256,256]{1,0:T(8,128)}, u32[]{:S(2)}) %copy-start.2) | copy-done | bytes 262168
  3.7 0.0 copy-start.3
  3.7 0.9 %copy-done.3 = f32[256,256]{1,0:T(8,128)S(1)} copy-done((f32[256,256]{1,0:T(8,128)S(1)}, f32[256,256]{1,0:T(8,128)}, u32[]{:S(2)}) %copy-start.3) | copy-done | bytes 262168
  4.6 0.0 copy-start.4
  4.6 0.8 %copy-done.4 = f32[64,250]{1,0:T(8,128)S(1)} copy-done((f32[64,250]{1,0:T(8,128)S(1)}, f32[64,250]{1,0:T(8,128)}, u32[]{:S(2)}) %copy-start.4) | copy-done | bytes 64024
  5.5 0.0 copy-start.5
  5.5 0.8 %copy-done.5 = f32[64,250]{1,0:T(8,128)S(1)} copy-done((f32[64,250]{1,0:T(8,128)S(1)}, f32[64,250]{1,0:T(8,128)}, u32[]{:S(2)}) %copy-start.5) | copy-done | bytes 64024
  6.3 0.0 copy-start.6
  6.3 0.8 %copy-done.6 = f32[64,250]{1,0:T(8,128)S(1)} copy-done((f32[64,250]{1,0:T(8,128)S(1)}, f32[64,250]{1,0:T(8,128)}, u32[]{:S(2)}) %copy-start.6) | copy-done | bytes 64024
  7.1 0.0 copy-start.7
  7.1 0.8 %copy-done.7 = f32[64,250]{1,0:T(8,128)S(1)} copy-done((f32[64,250]{1,0:T(8,128)S(1)}, f32[64,250]{1,0:T(8,128)}, u32[]{:S(2)}) %copy-start.7) | copy-done | bytes 64024
  8.0 0.0 copy-start.8
  8.0 0.8 %copy-done.8 = bf16[256,16]{1,0:T(8,128)(2,1)S(1)} copy-done((bf16[256,16]{1,0:T(8,128)(2,1)S(1)}, bf16[256,16]{1,0:T(8,128)(2,1)}, u32[]{:S(2)}) %copy-start.8) | copy-done | bytes 8216
  8.8 0.0 copy-start.9
  8.8 0.8 %copy-done.9 = bf16[64,512]{1,0:T(8,128)(2,1)S(1)} copy-done((bf16[64,512]{1,0:T(8,128)(2,1)S(1)}, bf16[64,512]{1,0:T(8,128)(2,1)}, u32[]{:S(2)}) %copy-start.9) | copy-done | bytes 65560
  9.7 0.0 copy-start.10
  9.7 0.8 %copy-done.10 = bf16[64,512]{1,0:T(8,128)(2,1)S(1)} copy-done((bf16[64,512]{1,0:T(8,128)(2,1)S(1)}, bf16[64,512]{1,0:T(8,128)(2,1)}, u32[]{:S(2)}) %copy-start.10) | copy-done | bytes 65560
  10.5 0.0 copy-start.11
  10.5 0.8 %copy-done.11 = bf16[128,64]{1,0:T(8,128)(2,1)S(1)} copy-done((bf16[128,64]{1,0:T(8,128)(2,1)S(1)}, bf16[128,64]{1,0:T(8,128)(2,1)}, u32[]{:S(2)}) %copy-start.11) | copy-done | bytes 16408
  11.3 0.0 copy-start.12
  11.3 0.8 %copy-done.12 = bf16[128,64]{1,0:T(8,128)(2,1)S(1)} copy-done((bf16[128,64]{1,0:T(8,128)(2,1)S(1)}, bf16[128,64]{1,0:T(8,128)(2,1)}, u32[]{:S(2)}) %copy-start.12) | copy-done | bytes 16408
  12.0 0.0 copy-start.13
  12.0 0.7 copy-done.13
  12.7 0.0 copy-start.14
  12.7 0.7 copy-done.14
  13.5 0.0 copy-start.15
  13.5 0.7 copy-done.15
  14.1 59.7 %shard_map.176 = (f32[64,250]{1,0:T(8,128)S(1)}, f32[64,250]{1,0:T(8,128)S(1)}) custom-call(f32[64,250]{1,0:T(8,128)S(1)} %copy-done.4, f32[64,250]{1,0:T(8,128)S(1)} %copy-done.5, f32[64,250]{1,0:T(8,128)S(1)} %copy-done.6, f32[64,250]{1,0:T(8,128)S(1)} %copy-done.7, f32[1,32]{1,0:T(1,128)S(1)} %bitcast.1, bf16[128,64]{1,0:T(8,128)(2,1)S(1)} %copy-done.12, ...), custom_call_target="tpu_custom_call" | custom-call | tf_op jit(solution)/shard_map/pallas_call | solution.py:491
  73.9 0.6 copy.21
  74.5 0.6 copy.22
Async XLA Ops:
  0.6 1.0 %copy-start = (bf16[512,512]{1,0:T(8,128)(2,1)S(1)}, bf16[512,512]{1,0:T(8,128)(2,1)}, u32[]{:S(2)}) copy-start(bf16[512,512]{1,0:T(8,128)(2,1)} %constant.32.clone.refs_15_) | copy-start | bytes 1572868
  1.7 1.0 %copy-start.1 = (bf16[512,512]{1,0:T(8,128)(2,1)S(1)}, bf16[512,512]{1,0:T(8,128)(2,1)}, u32[]{:S(2)}) copy-start(bf16[512,512]{1,0:T(8,128)(2,1)} %constant.31.clone.refs_14_) | copy-start | bytes 1572868
  2.7 0.9 %copy-start.2 = (f32[256,256]{1,0:T(8,128)S(1)}, f32[256,256]{1,0:T(8,128)}, u32[]{:S(2)}) copy-start(f32[256,256]{1,0:T(8,128)} %constant.27.clone.refs_10_) | copy-start | bytes 786436
  3.7 0.9 %copy-start.3 = (f32[256,256]{1,0:T(8,128)S(1)}, f32[256,256]{1,0:T(8,128)}, u32[]{:S(2)}) copy-start(f32[256,256]{1,0:T(8,128)} %constant.26.clone.refs_9_) | copy-start | bytes 786436
  4.6 0.8 %copy-start.4 = (f32[64,250]{1,0:T(8,128)S(1)}, f32[64,250]{1,0:T(8,128)}, u32[]{:S(2)}) copy-start(f32[64,250]{1,0:T(8,128)} %refs_0_.1) | copy-start | bytes 192004
  5.5 0.8 %copy-start.5 = (f32[64,250]{1,0:T(8,128)S(1)}, f32[64,250]{1,0:T(8,128)}, u32[]{:S(2)}) copy-start(f32[64,250]{1,0:T(8,128)} %refs_1_.1) | copy-start | bytes 192004
  6.3 0.8 %copy-start.6 = (f32[64,250]{1,0:T(8,128)S(1)}, f32[64,250]{1,0:T(8,128)}, u32[]{:S(2)}) copy-start(f32[64,250]{1,0:T(8,128)} %refs_2_.1) | copy-start | bytes 192004
  7.1 0.8 %copy-start.7 = (f32[64,250]{1,0:T(8,128)S(1)}, f32[64,250]{1,0:T(8,128)}, u32[]{:S(2)}) copy-start(f32[64,250]{1,0:T(8,128)} %refs_3_.1) | copy-start | bytes 192004
  8.0 0.8 %copy-start.8 = (bf16[256,16]{1,0:T(8,128)(2,1)S(1)}, bf16[256,16]{1,0:T(8,128)(2,1)}, u32[]{:S(2)}) copy-start(bf16[256,16]{1,0:T(8,128)(2,1)} %constant.30.clone.refs_13_) | copy-start | bytes 24580
  8.8 0.8 %copy-start.9 = (bf16[64,512]{1,0:T(8,128)(2,1)S(1)}, bf16[64,512]{1,0:T(8,128)(2,1)}, u32[]{:S(2)}) copy-start(bf16[64,512]{1,0:T(8,128)(2,1)} %constant.29.clone.refs_12_) | copy-start | bytes 196612
  9.7 0.8 %copy-start.10 = (bf16[64,512]{1,0:T(8,128)(2,1)S(1)}, bf16[64,512]{1,0:T(8,128)(2,1)}, u32[]{:S(2)}) copy-start(bf16[64,512]{1,0:T(8,128)(2,1)} %constant.28.clone.refs_11_) | copy-start | bytes 196612
  10.5 0.8 %copy-start.11 = (bf16[128,64]{1,0:T(8,128)(2,1)S(1)}, bf16[128,64]{1,0:T(8,128)(2,1)}, u32[]{:S(2)}) copy-start(bf16[128,64]{1,0:T(8,128)(2,1)} %constant.23.clone.refs_6_) | copy-start | bytes 49156
  11.3 0.8 %copy-start.12 = (bf16[128,64]{1,0:T(8,128)(2,1)S(1)}, bf16[128,64]{1,0:T(8,128)(2,1)}, u32[]{:S(2)}) copy-start(bf16[128,64]{1,0:T(8,128)(2,1)} %constant.22.clone.refs_5_) | copy-start | bytes 49156
  12.0 0.7 copy-start.13
  12.7 0.7 copy-start.14
  13.5 0.7 copy-start.15

commit v3 on v2

--- a/solution.py
+++ b/solution.py
@@ -519,7 +519,7 @@
         compiler_params=pltpu.CompilerParams(
             collective_id=0, has_side_effects=True, vmem_limit_bytes=48 << 20
         ),
-    )(*grid, *consts, legendre)
+    )(*[pltpu.with_memory_space_constraint(x, pltpu.HBM) for x in (*grid, *consts, legendre)])
 
 
 def solution(mesh):

time: 75.9 us -> 61.5 us (0.81)
  local copies, waits for them, and re-layouts: 14.7 us -> 1.26 us
    unnamed x34 -> x2, local copies, waits for them, and re-layouts: 14.7 us -> 1.26 us
where the time goes in v3:
time: 61.5 us
  Pallas kernels  59.6 us (97%)
  local copies, waits for them, and re-layouts  1.26 us (2%)
  between operations  0.64 us (1%)
    pallas_call x1, Pallas kernels, per_device(): pl.pallas_call(kernel, out_shape=(grid_shape, grid_shape), in_specs=[hbm]...  59.6 us
    unnamed x2, local copies, waits for them, and re-layouts  1.26 us

profile of v3, /device:TPU:2, one launch (start us, length us, event | category | flops | bytes accessed | tf_op | source)
XLA Modules:
  0.0 61.5 jit_solution(7831646638027756067)
XLA Ops:
  0.6 59.6 %shard_map.176 = (f32[64,250]{1,0:T(8,128)S(1)}, f32[64,250]{1,0:T(8,128)S(1)}) custom-call(f32[64,250]{1,0:T(8,128)} %refs_0_.1, f32[64,250]{1,0:T(8,128)} %refs_1_.1, f32[64,250]{1,0:T(8,128)} %refs_2_.1, f32[64,250]{1,0:T(8,128)} %refs_3_.1, f32[1,32]{1,0:T(1,128)} %bitcast.1, bf16[128,64]{1,0:T(8,128)(2,1)} %constant.22.clone.refs_5_, ...), custom_call_target="tpu_custom_call" | custom-call | tf_op jit(solution)/shard_map/pallas_call | solution.py:491
  60.2 0.6 %copy.21 = f32[64,250]{1,0:T(8,128)} copy(f32[64,250]{1,0:T(8,128)S(1)} %get-tuple-element.4) | data formatting | bytes 128000
  60.8 0.6 %copy.22 = f32[64,250]{1,0:T(8,128)} copy(f32[64,250]{1,0:T(8,128)S(1)} %get-tuple-element.5) | data formatting | bytes 128000

commit v4 on v3

--- a/solution.py
+++ b/solution.py
@@ -51,9 +51,13 @@
         return scale * np.cos(phi) * real, scale * np.sin(phi) * real
 
     cos, sin = over_j(np.stack([tau, -tau]), 1)
-    inner = np.concatenate(
+    block = np.concatenate(
         [np.concatenate([cos, sin], axis=2), np.concatenate([-sin, cos], axis=2)], axis=1
-    ).reshape(64, 512)
+    )
+    inner = np.zeros((2, 512, 128))
+    for member in range(2):
+        inner[member, :, 32 * member : 32 * (member + 1)] = block[member].T
+    inner = inner.reshape(1024, 128)
     row = np.stack([(PAIRS * s) // 128, (PAIRS * s + 1) // 128])
     row = np.concatenate([row, row + 1], axis=1)
     pick = (row[..., None] == tau).reshape(256, 16)
@@ -117,42 +121,63 @@
     return jnp.concatenate([x, x], axis=0)
 
 
-def forward_row(x, spread, twist, inner, pick):
-    y = three(dot, spread, split(x))
+def forward_rows(x, spread, twist, inner, pick):
+    y = dot(spread[0], x) + dot(spread[1], x)
     re, im = twice(y[:LON_DEV]), twice(y[LON_DEV:])
-    message = None
+    waves = None
     for member in range(2):
         rows = slice(128 * member, 128 * (member + 1))
-        cos, sin = twist[0][rows], twist[1][rows]
+        cos, sin = (jnp.concatenate([t[rows]] * 3, axis=1) for t in twist)
         if member == 0:
             z = [re * cos + im * sin, im * cos - re * sin]
         else:
             z = [re * cos - im * sin, -(im * cos + re * sin)]
-        z = split(jnp.concatenate(z, axis=1))
-        cols = slice(32 * member, 32 * (member + 1))
-        waves = three(dot_nt, (inner[0][cols], inner[1][cols]), z).astype(bf16)
-        values = dot(pick[rows], jnp.concatenate([waves[:16], waves[16:]], axis=1))
+        z = [
+            jnp.concatenate([part[:, 256 * f : 256 * (f + 1)] for f in range(3)], axis=0)
+            for part in z
+        ]
+        cols = slice(512 * member, 512 * (member + 1))
+        term = three(dot, split(jnp.concatenate(z, axis=1)), (inner[0][cols], inner[1][cols]))
+        waves = term if waves is None else waves + term
+    waves = [waves[128 * f : 128 * (f + 1)].T.astype(bf16) for f in range(3)]
+    messages = [None] * 3
+    for member in range(2):
+        rows = slice(128 * member, 128 * (member + 1))
+        first = 32 * member
+        parts = [
+            w[first + 16 * part : first + 16 * (part + 1)] for w in waves for part in range(2)
+        ]
+        values = dot(pick[rows], jnp.concatenate(parts, axis=1))
         straight, wrapped = lane_masks(member)
-        for part in range(2):
-            slot = part * 2 + member
-            cols = slice(128 * part, 128 * (part + 1))
-            own = jnp.where(
-                straight, values[:LON_DEV, cols], jnp.where(wrapped, values[LON_DEV:, cols], 0.0)
-            )
-            own = pltpu.roll(own, 32 * slot, 1) if slot else own
-            message = own if message is None else message + own
-    return message
-
-
-def column_products(rows, lon):
+        for f in range(3):
+            for part in range(2):
+                slot = part * 2 + member
+                cols = slice(128 * (2 * f + part), 128 * (2 * f + part + 1))
+                own = jnp.where(
+                    straight,
+                    values[:LON_DEV, cols],
+                    jnp.where(wrapped, values[LON_DEV:, cols], 0.0),
+                )
+                own = pltpu.roll(own, 32 * slot, 1) if slot else own
+                messages[f] = own if messages[f] is None else messages[f] + own
+    return messages
+
+
+def pair_order(lon):
     r = iota((16 * GROUPS, 128), 0)
     member, part = (r >> 3) & 1, (r >> 2) & 1
     target = lon * PAIRS + 64 * part + 33 * member + 4 * (r >> 4) + (r & 3)
-    order = (((iota((16 * GROUPS, 128), 1) - target) & 127) == 0).astype(f32).astype(bf16)
-    q = dot_nt(order, rows.astype(bf16)).astype(bf16)
+    return (((iota((16 * GROUPS, 128), 1) - target) & 127) == 0).astype(f32).astype(bf16)
+
+
+def latitude_copies():
     source, lane = iota((64, 256), 0), iota((64, 256), 1)
     same = ((source >> 5) == (lane >> 7)) & ((source & 31) == (lane & 31))
-    wide = dot(q, same.astype(f32).astype(bf16))
+    return same.astype(f32).astype(bf16)
+
+
+def column_products(rows, order, copies):
+    wide = dot(dot_nt(order, rows.astype(bf16)).astype(bf16), copies)
     own = ((iota(wide.shape, 1) >> 5) & 3) == (iota(wide.shape, 0) & 3)
     return jnp.where(own, wide, 0.0)
 
@@ -212,31 +237,37 @@
     return (same & (((c - target) & 127) == 0)).astype(f32).astype(bf16)
 
 
-def inverse_row(c, spread_t, twist, back):
+def inverse_both(fields, spread_t, twist, back):
     mean = (iota((LON_DEV, 128), 0) == 0) & (iota((LON_DEV, 128), 1) == 0)
     total = None
     for member in range(2):
         straight, wrapped = lane_masks(member)
-        stack = []
-        for part in range(2):
-            slot = part * 2 + member
-            x = pltpu.roll(c, 128 - 32 * slot, 1) if slot else c
-            if member == 0:
-                x = jnp.where(mean, 0.5 * x, x)
-            stack += [jnp.where(straight, x, 0.0), jnp.where(wrapped, x, 0.0)]
-        x = split(jnp.concatenate(stack, axis=0).T)
+        turned = []
+        for c in fields:
+            stack = []
+            for part in range(2):
+                slot = part * 2 + member
+                x = pltpu.roll(c, 128 - 32 * slot, 1) if slot else c
+                if member == 0:
+                    x = jnp.where(mean, 0.5 * x, x)
+                stack += [jnp.where(straight, x, 0.0), jnp.where(wrapped, x, 0.0)]
+            turned.append(jnp.concatenate(stack, axis=0).T)
         rows = slice(256 * member, 256 * (member + 1))
-        b = three(dot, x, (back[0][rows], back[1][rows]))
-        re, im = b[:, :256], b[:, 256:]
+        b = three(dot, split(jnp.concatenate(turned, axis=0)), (back[0][rows], back[1][rows]))
         rows = slice(128 * member, 128 * (member + 1))
         cos, sin = twist[0][rows], twist[1][rows]
-        z = [re * cos - im * sin, re * sin + im * cos]
-        z = [part[:LON_DEV] + part[LON_DEV:] for part in z]
+        z = [[], []]
+        for f in range(2):
+            re, im = b[128 * f : 128 * (f + 1), :256], b[128 * f : 128 * (f + 1), 256:]
+            for part, x in enumerate((re * cos - im * sin, re * sin + im * cos)):
+                z[part].append(x[:LON_DEV] + x[LON_DEV:])
+        z = [jnp.concatenate(part, axis=1) for part in z]
         total = z if total is None else [total[0] + z[0], total[1] - z[1]]
     return three(dot, spread_t, split(jnp.concatenate(total, axis=0)))
 
 
 CONSTS = 11
+LAG = 2
 
 
 def kernel(*refs):
@@ -245,8 +276,8 @@
     legendre, out_height, out_divergence, *refs = refs
     grid, refs = refs[:5], refs[5:]
     consts, refs = refs[:CONSTS], refs[CONSTS:]
-    table, field_buf, tx1, rx1, tx2, rx2, tx4, rx4, tx5, rx5, *refs = refs
-    columns, sums, sibling_sums, chip_tx, chip_rx, solved, message, *refs = refs
+    table, field_buf, row_buf, tx1, rx1, tx2, rx2, tx4, rx4, tx5, rx5, *refs = refs
+    tails, order, copies, orders, columns, sums, sibling_sums, chip_tx, chip_rx, solved, message, *refs = refs
     in_sem, table_sem, send_sem, recv_sem, own_sem, lat_send, lat_recv = refs
     lon, lat = lax.axis_index("lon"), lax.axis_index("lat")
     core = lax.rem(lat, 2)
@@ -332,7 +363,8 @@
         field_buf[0:HALF, 0:SPAN] = even
         field_buf[HALF:, 0:SPAN] = odd
         for h in range(2):
-            tx1[pl.ds(2 * f + h, LON_DEV, stride=6), :] = field_buf[:, 128 * h : 128 * (h + 1)]
+            row_buf[pl.ds(2 * f + h, LON_DEV, stride=6), :] = field_buf[:, 128 * h : 128 * (h + 1)]
+    tx1[...] = row_buf[...].astype(bf16)
 
     pl.semaphore_wait(barrier, LON_DEV + 1)
     exchange_start(0, tx1, rx1)
@@ -343,33 +375,42 @@
     pick = consts[8]
     exchange_wait(0, tx1, rx1)
 
+    row_buf[...] = rx1[...].astype(f32)
+    x = jnp.concatenate([row_buf[pl.ds(c, LON_DEV, stride=6), :] for c in range(6)], axis=1)
+    for f, rows in enumerate(forward_rows(x.astype(bf16), spread, twist, inner, pick)):
+        tx2[pl.ds(f, LON_DEV, stride=3), :] = rows
+    exchange_start(1, tx2, rx2)
+
+    def prepare(g, _):
+        table_copy(g).wait()
+        last = table[pl.ds(GROUP * g, GROUP), :, SLOTS - 1 : SLOTS].reshape(128, 1).astype(f32)
+        last = jnp.where(iota((128, 128), 1) == 0, jnp.broadcast_to(last, (128, 128)), 0.0)
+        tails[g] = last.astype(bf16)
+        orders[g] = lane_order(lon, g)
+        return 0
+
+    lax.fori_loop(0, GROUPS, prepare, 0)
+    order[...] = pair_order(lon)
+    copies[...] = latitude_copies()
+    message[...] = jnp.zeros_like(message)
+    exchange_wait(1, tx2, rx2)
+
     for f in range(3):
-        x = jnp.concatenate([rx1[pl.ds(2 * f + h, LON_DEV, stride=6), :] for h in range(2)], axis=1)
-        tx2[pl.ds(f, LON_DEV, stride=3), :] = forward_row(x, spread, twist, inner, pick)
-    exchange_start(1, tx2, rx2)
-    exchange_wait(1, tx2, rx2)
-
-    for f in range(3):
-        wide = column_products(rx2[pl.ds(f, LON_DEV, stride=3), :], lon).astype(bf16)
+        rows = rx2[pl.ds(f, LON_DEV, stride=3), :]
+        wide = column_products(rows, order[...], copies[...]).astype(bf16)
         for g in range(GROUPS):
             for par in range(2):
                 columns[g, 16 * (par * 3 + f) : 16 * (par * 3 + f + 1), :] = wide[
                     16 * g : 16 * (g + 1), 128 * par : 128 * (par + 1)
                 ]
 
-    def table_tail(g):
-        last = table[pl.ds(GROUP * g, GROUP), :, SLOTS - 1 : SLOTS].reshape(128, 1).astype(f32)
-        return jnp.where(iota((128, 128), 1) == 0, jnp.broadcast_to(last, (128, 128)), 0.0).astype(
-            bf16
-        )
-
     def table_tile(g, t):
         return table[pl.ds(GROUP * g, GROUP), :, TILE * t : TILE * (t + 1)].reshape(128, TILE)
 
     def tiles(g):
         for t in range(TILES):
             yield TILE * t, TILE, table_tile(g, t)
-        yield TILE * TILES, 128, table_tail(g)
+        yield TILE * TILES, 128, tails[g]
 
     def sibling_copy(g):
         return pltpu.make_async_remote_copy(
@@ -395,7 +436,6 @@
         )
 
     def forward_group(g):
-        table_copy(g).wait()
         pair_first = lon * PAIRS + GROUP * g
         for first, width, rhs in tiles(g):
             both = partial_solve(dot(columns[g], rhs), pair_first, first)
@@ -425,22 +465,21 @@
             term = dot_nt(rhs, inverse_rows(both, pair_first, first))
             total = term if total is None else total + term
         high, low = split(own_pair(total))
-        order = lane_order(lon, g)
-        message[...] += dot(high, order) + dot(low, order)
+        message[...] += dot(high, orders[g]) + dot(low, orders[g])
 
     def forward_step(t, _):
         forward_group(t)
 
-        @pl.when(t > 0)
+        @pl.when(t >= LAG)
         def _():
-            sibling_sum(t - 1)
+            sibling_sum(t - LAG)
 
         return 0
 
     lax.fori_loop(0, GROUPS, forward_step, 0)
-    sibling_sum(GROUPS - 1)
-
-    message[...] = jnp.zeros_like(message)
+    for g in range(GROUPS - LAG, GROUPS):
+        sibling_sum(g)
+
     across_sum(0)
 
     def inverse_step(t, _):
@@ -461,10 +500,10 @@
     exchange_start(2, tx4, rx4)
     exchange_wait(2, tx4, rx4)
 
-    for field in range(2):
-        grid = inverse_row(rx4[pl.ds(field, LON_DEV, stride=2), :], spread_t, twist, back)
-        for h in range(2):
-            tx5[pl.ds(2 * field + h, LON_DEV, stride=4), :] = grid[:, 128 * h : 128 * (h + 1)]
+    fields = [rx4[pl.ds(field, LON_DEV, stride=2), :] for field in range(2)]
+    grid = inverse_both(fields, spread_t, twist, back)
+    for c in range(4):
+        tx5[pl.ds(c, LON_DEV, stride=4), :] = grid[:, 128 * c : 128 * (c + 1)]
     exchange_start(3, tx5, rx5)
     exchange_wait(3, tx5, rx5)
     for field, out in enumerate((out_height, out_divergence)):
@@ -484,8 +523,8 @@
     vmem, hbm = pl.BlockSpec(memory_space=pltpu.VMEM), pl.BlockSpec(memory_space=pltpu.HBM)
     grid_shape = jax.ShapeDtypeStruct(height.shape, f32)
 
-    def pair(rows):
-        return [pltpu.VMEM((LON_DEV * rows, 128), f32)] * 2
+    def pair(rows, dtype=f32):
+        return [pltpu.VMEM((LON_DEV * rows, 128), dtype)] * 2
 
     wide = 128 * pl.cdiv(SLOTS, 128)
     return pl.pallas_call(
@@ -497,10 +536,15 @@
             *[pltpu.VMEM(x.shape, x.dtype) for x in (*grid, *consts)],
             pltpu.VMEM((PAIRS, HALF, SLOTS), bf16),
             pltpu.VMEM((2 * HALF, 256), f32),
-            *pair(6),
+            pltpu.VMEM((LON_DEV * 6, 128), f32),
+            *pair(6, bf16),
             *pair(3),
             *pair(2),
             *pair(4),
+            pltpu.VMEM((GROUPS, 128, 128), bf16),
+            pltpu.VMEM((16 * GROUPS, 128), bf16),
+            pltpu.VMEM((2 * HALF, 256), bf16),
+            pltpu.VMEM((GROUPS, 64, 512), bf16),
             pltpu.VMEM((GROUPS, 96, 128), bf16),
             pltpu.VMEM((GROUPS, 2, 8, wide), f32),
             pltpu.VMEM((GROUPS, 8, wide), f32),

time: 61.5 us -> 60 us (0.976)
  Pallas kernels: 59.6 us -> 58 us
    pallas_call x1, Pallas kernels: 59.6 us -> 58 us  [per_device(): pl.pallas_call(kernel, out_shape=(grid_shape, grid_shape), in_specs=[hbm]...]
where the time goes in v4:
time: 60 us; the launch traced here: 59.9 us
  Pallas kernels  58 us (97%)
  local copies, waits for them, and re-layouts  1.26 us (2%)
  between operations  0.64 us (1%)
    pallas_call x1, Pallas kernels, per_device(): pl.pallas_call(kernel, out_shape=(grid_shape, grid_shape), in_specs=[hbm]...  58 us
    unnamed x2, local copies, waits for them, and re-layouts  1.26 us

profile of v4, /device:TPU:2, one launch (start us, length us, event | category | flops | bytes accessed | tf_op | source)
XLA Modules:
  0.0 59.9 jit_solution(9090403334936138263)
XLA Ops:
  0.6 58.0 %shard_map.176 = (f32[64,250]{1,0:T(8,128)S(1)}, f32[64,250]{1,0:T(8,128)S(1)}) custom-call(f32[64,250]{1,0:T(8,128)} %refs_0_.1, f32[64,250]{1,0:T(8,128)} %refs_1_.1, f32[64,250]{1,0:T(8,128)} %refs_2_.1, f32[64,250]{1,0:T(8,128)} %refs_3_.1, f32[1,32]{1,0:T(1,128)} %bitcast.1, bf16[128,64]{1,0:T(8,128)(2,1)} %constant.22.clone.refs_5_, ...), custom_call_target="tpu_custom_call" | custom-call | tf_op jit(solution)/shard_map/pallas_call | solution.py:530
  58.6 0.6 %copy.21 = f32[64,250]{1,0:T(8,128)} copy(f32[64,250]{1,0:T(8,128)S(1)} %get-tuple-element.4) | data formatting | bytes 128000
  59.3 0.6 %copy.22 = f32[64,250]{1,0:T(8,128)} copy(f32[64,250]{1,0:T(8,128)S(1)} %get-tuple-element.5) | data formatting | bytes 128000

commit v5 on v4

--- a/solution.py
+++ b/solution.py
@@ -273,7 +273,7 @@
 def kernel(*refs):
     grid_in, refs = refs[:5], refs[5:]
     consts_in, refs = refs[:CONSTS], refs[CONSTS:]
-    legendre, out_height, out_divergence, *refs = refs
+    legendre, out, *refs = refs
     grid, refs = refs[:5], refs[5:]
     consts, refs = refs[:CONSTS], refs[CONSTS:]
     table, field_buf, row_buf, tx1, rx1, tx2, rx2, tx4, rx4, tx5, rx5, *refs = refs
@@ -506,9 +506,9 @@
         tx5[pl.ds(c, LON_DEV, stride=4), :] = grid[:, 128 * c : 128 * (c + 1)]
     exchange_start(3, tx5, rx5)
     exchange_wait(3, tx5, rx5)
-    for field, out in enumerate((out_height, out_divergence)):
-        out[:, 0:128] = rx5[pl.ds(2 * field, LON_DEV, stride=4), :]
-        out[:, 128:SPAN] = rx5[pl.ds(2 * field + 1, LON_DEV, stride=4), :][:, : SPAN - 128]
+    for field in range(2):
+        for h in range(2):
+            out[field, :, 128 * h : 128 * (h + 1)] = rx5[pl.ds(2 * field + h, LON_DEV, stride=4), :]
 
     for phase, tx in enumerate((tx1, tx2, tx4, tx5)):
         exchange_sent(phase, tx)
@@ -527,11 +527,11 @@
         return [pltpu.VMEM((LON_DEV * rows, 128), dtype)] * 2
 
     wide = 128 * pl.cdiv(SLOTS, 128)
-    return pl.pallas_call(
+    raw = pl.pallas_call(
         kernel,
-        out_shape=(grid_shape, grid_shape),
+        out_shape=jax.ShapeDtypeStruct((2, LON_DEV, 256), f32),
         in_specs=[hbm] * (len(grid) + len(consts) + 1),
-        out_specs=(vmem, vmem),
+        out_specs=vmem,
         scratch_shapes=[
             *[pltpu.VMEM(x.shape, x.dtype) for x in (*grid, *consts)],
             pltpu.VMEM((PAIRS, HALF, SLOTS), bf16),
@@ -564,6 +564,7 @@
             collective_id=0, has_side_effects=True, vmem_limit_bytes=48 << 20
         ),
     )(*[pltpu.with_memory_space_constraint(x, pltpu.HBM) for x in (*grid, *consts, legendre)])
+    return raw[0, :, :SPAN], raw[1, :, :SPAN]
 
 
 def solution(mesh):

time: 60 us -> 59.4 us (0.990)
  local copies, waits for them, and re-layouts: 1.26 us -> 0.66 us
    unnamed x2 -> x0, local copies, waits for them, and re-layouts: 1.26 us -> none
    squeeze x0 -> x1, local copies, waits for them, and re-layouts: none -> 0.66 us  [per_device(): return (raw[0, :, :SPAN], raw[1, :, :SPAN])]
where the time goes in v5:
time: 59.4 us; the launch traced here: 59.3 us
  Pallas kernels  58 us (98%)
  local copies, waits for them, and re-layouts  0.66 us (1%)
  between operations  0.64 us (1%)
    pallas_call x1, Pallas kernels, per_device(): pl.pallas_call(kernel, out_shape=jax.ShapeDtypeStruct((2, LON_DEV, 256),...  58 us

profile of v5, /device:TPU:2, one launch (start us, length us, event | category | flops | bytes accessed | tf_op | source)
XLA Modules:
  0.0 59.3 jit_solution(18358048184015832408)
XLA Ops:
  0.6 58.0 %shard_map.176 = f32[2,64,256]{2,1,0:T(8,128)S(1)} custom-call(f32[64,250]{1,0:T(8,128)} %refs_0_.1, f32[64,250]{1,0:T(8,128)} %refs_1_.1, f32[64,250]{1,0:T(8,128)} %refs_2_.1, f32[64,250]{1,0:T(8,128)} %refs_3_.1, f32[1,32]{1,0:T(1,128)} %bitcast.5, bf16[128,64]{1,0:T(8,128)(2,1)} %constant.22.clone.refs_5_, bf16[128,64]{1,0:T(8,128)(2,1)} %constant.23.clone.refs_6_, ...), custom_call_target="tpu_custom_call" | custom-call | tf_op jit(solution)/shard_map/pallas_call | solution.py:530
  58.6 0.7 %slice_bitcast_fusion = (f32[64,250]{1,0:T(8,128)}, f32[64,250]{1,0:T(8,128)}) fusion(f32[2,64,256]{2,1,0:T(8,128)S(1)} %shard_map.176), kind=kLoop, calls=%fused_computation | loop fusion | bytes 256000 | tf_op jit(solution)/shard_map/squeeze | solution.py:567

commit v6 on v5

--- a/solution.py
+++ b/solution.py
@@ -267,7 +267,7 @@
 
 
 CONSTS = 11
-LAG = 2
+LAG = 1
 
 
 def kernel(*refs):

time: 59.4 us -> 58.8 us (0.990)
  Pallas kernels: 58 us -> 57.4 us
where the time goes in v6:
time: 58.8 us; the launch traced here: 58.7 us
  Pallas kernels  57.4 us (98%)
  local copies, waits for them, and re-layouts  0.66 us (1%)
  between operations  0.64 us (1%)
    pallas_call x1, Pallas kernels, per_device(): pl.pallas_call(kernel, out_shape=jax.ShapeDtypeStruct((2, LON_DEV, 256),...  57.4 us

profile of v6, /device:TPU:2, one launch (start us, length us, event | category | flops | bytes accessed | tf_op | source)
XLA Modules:
  0.0 58.7 jit_solution(8990961504203553406)
XLA Ops:
  0.6 57.4 %shard_map.176 = f32[2,64,256]{2,1,0:T(8,128)S(1)} custom-call(f32[64,250]{1,0:T(8,128)} %refs_0_.1, f32[64,250]{1,0:T(8,128)} %refs_1_.1, f32[64,250]{1,0:T(8,128)} %refs_2_.1, f32[64,250]{1,0:T(8,128)} %refs_3_.1, f32[1,32]{1,0:T(1,128)} %bitcast.5, bf16[128,64]{1,0:T(8,128)(2,1)} %constant.22.clone.refs_5_, bf16[128,64]{1,0:T(8,128)(2,1)} %constant.23.clone.refs_6_, ...), custom_call_target="tpu_custom_call" | custom-call | tf_op jit(solution)/shard_map/pallas_call | solution.py:530
  58.0 0.7 %slice_bitcast_fusion = (f32[64,250]{1,0:T(8,128)}, f32[64,250]{1,0:T(8,128)}) fusion(f32[2,64,256]{2,1,0:T(8,128)S(1)} %shard_map.176), kind=kLoop, calls=%fused_computation | loop fusion | bytes 256000 | tf_op jit(solution)/shard_map/squeeze | solution.py:567
